TPU v7x, 256 devices: a whole 4x4x8 slice. The times are simulated.
256 devices in a mesh: seq: 16 (over z_lo, y, core), wide: 16 (over x, z_hi).
Axes of the slice: x: 4, y: 4, z: 8 (z_hi: 4, z_lo: 2; z = z_hi * 2 + z_lo), core: 2. Of those that a mesh axis runs over, the one named last changes fastest.
Arguments:
- qkv_proj: bfloat16 [3, 2, 16384, 8192], P(None, None, ('seq', 'wide')), may hold values from -6 to 6
- conv_kernel: float32 [3, 4, 8192], replicated, may hold values from -3 to 3
- qk_gain: float32 [2, 16, 512], P(None, 'wide'), may hold values from 0.4 to 2.5
- fast_init: float32 [3, 16, 512, 512], P(None, 'wide'), may hold values from -0.25 to 0.25
- step_size: float32 [16], P('wide'), may hold values from 0.2 to 1
Outputs:
- fast_out: bfloat16 [2, 16384, 8192], P(None, 'seq', 'wide')
All inputs are finite; a program needn't handle non-finite values.
Results may differ from a plain program's by a relative error of at most 0.004.
Values may be sent and summed in bfloat16 or wider, within the bound.
No kernel may reach another device: no remote copies, remote signals or barrier semaphores. Data moves between devices by JAX's collectives and lax.ppermute only.
A program may use at most 128 MiB of HBM per device.

v0:
```python
import jax
import jax.numpy as jnp
from jax import lax
from jax.sharding import PartitionSpec as P

HEAD = 512
GROUPS = 2
KW = 4


EPS = 1e-06
BETA = 0.6


def from_behind(value, axis, steps):
    count = lax.axis_size(axis)
    pairs = [(source, (source + steps) % count) for source in range(count)]
    return lax.ppermute(value, axis, pairs)


def cut_along(value, dim, devices):
    before, after = (value.shape[:dim], value.shape[dim + 1 :])
    return jnp.moveaxis(value.reshape(*before, devices, -1, *after), dim, 0)


def cut_rows(length, count):
    lap = length // count
    if lap >= 8:
        lap -= lap % 8
    return [lap * k for k in range(1, count)]


def laid_out(parts, dim):
    dims = list(parts.shape[1:])
    dims[dim] *= parts.shape[0]
    return jnp.moveaxis(parts, 0, dim).reshape(dims)


def several_exchanges(value, axis, pieces, split_dim, concat_dim):
    parts = cut_along(value, split_dim, lax.axis_size(axis))
    cut = max(range(1, max(2, parts.ndim - 1)), key=lambda d: parts.shape[d])
    outs = []
    for slab in jnp.split(parts, cut_rows(parts.shape[cut], pieces), axis=cut):
        if slab.size:
            outs.append(lax.all_to_all(slab, axis, split_axis=0, concat_axis=0, tiled=True))
    return laid_out(jnp.concatenate(outs, axis=cut), concat_dim)


def summed_on_arrival(value, axis, dim):
    devices = lax.axis_size(axis)
    parts = lax.all_to_all(cut_along(value, dim, devices), axis, 0, 0, tiled=True)
    return jnp.sum(parts.astype(jnp.float32), axis=0)


def matmul(left, right):
    return jnp.dot(left, right, preferred_element_type=jnp.float32)


def contract_rows(left, right):
    return lax.dot_general(
        left, right, (((0,), (0,)), ((), ())), preferred_element_type=jnp.float32
    )


def contract_cols(left, right):
    return lax.dot_general(
        left, right, (((1,), (1,)), ((), ())), preferred_element_type=jnp.float32
    )


def rms_rows(values_in):
    values_in = values_in.astype(jnp.float32)
    return values_in * lax.rsqrt(jnp.mean(values_in * values_in, axis=-1, keepdims=True) + EPS)


def normalize_columns(moment):
    return moment * lax.rsqrt(jnp.mean(moment * moment, axis=1, keepdims=True) + EPS)


def local_gradients(weights, keys_in, values_in):
    narrow = weights.astype(jnp.bfloat16)
    gate_pre = matmul(keys_in, narrow[0])
    up_pre = matmul(keys_in, narrow[1])
    sigmoid_gate = jax.nn.sigmoid(gate_pre)
    gate_act = gate_pre * sigmoid_gate
    hidden = (gate_act * up_pre).astype(jnp.bfloat16)
    back_hidden = contract_cols(values_in, narrow[2])
    g_down = contract_rows(hidden, values_in)
    err_gate = (
        back_hidden * up_pre * sigmoid_gate * (1.0 + gate_pre * (1.0 - sigmoid_gate))
    ).astype(jnp.bfloat16)
    err_up = (back_hidden * gate_act).astype(jnp.bfloat16)
    g_gate = contract_rows(keys_in, err_gate)
    g_up = contract_rows(keys_in, err_up)
    return jnp.stack([g_gate, g_up, g_down])


def apply_fast(weights, queries):
    narrow = weights.astype(jnp.bfloat16)
    hidden = (jax.nn.silu(matmul(queries, narrow[0])) * matmul(queries, narrow[1])).astype(
        jnp.bfloat16
    )
    return matmul(hidden, narrow[2])


def conv_rows(extended, kernel, row_count):
    rim_width = KW - 1
    summed = jnp.zeros(extended.shape[:2] + (row_count, extended.shape[3]), jnp.float32)
    for tap_index in range(KW):
        begin = rim_width - tap_index
        summed = summed + kernel[:, tap_index][:, None, None, :] * extended[
            :, :, begin : begin + row_count, :
        ].astype(jnp.float32)
    return summed


def local(qkv_proj, conv_kernel, qk_gain, fast_init, step_size):
    row_count = qkv_proj.shape[2]
    rim_width = KW - 1
    tail_rows = qkv_proj[:, :, row_count - rim_width :, :]
    before = from_behind(tail_rows, ("seq", "wide"), 1)
    shifted = jnp.concatenate([jnp.zeros_like(before[:, :1]), before[:, :-1]], axis=1)
    leading = lax.axis_index(("seq", "wide")) == 0
    rim_rows = jnp.where(leading, shifted, before)
    extended = jnp.concatenate([rim_rows, qkv_proj], axis=2)
    activated = jax.nn.silu(conv_rows(extended, conv_kernel, row_count)).astype(jnp.bfloat16)
    regrouped = several_exchanges(activated, "wide", 2, 3, 2)
    seq_count = lax.axis_size("seq")
    group_total = row_count * lax.axis_size("wide") * seq_count
    gains = qk_gain[:, 0]
    weights = fast_init[:, 0]
    step_scale = step_size[0] * HEAD ** (-0.5)
    momentum = None
    outputs = []
    for group_index in range(GROUPS):
        group_data = regrouped[:, group_index]
        queries = (rms_rows(group_data[0]) * gains[0]).astype(jnp.bfloat16)
        keys_in = (rms_rows(group_data[1]) * gains[1]).astype(jnp.bfloat16)
        values_in = group_data[2] * (-1.0 / group_total)
        gradients = local_gradients(weights, keys_in, values_in)
        partial_value = summed_on_arrival(gradients.astype(jnp.bfloat16), "seq", 2)
        if momentum is None:
            momentum = jnp.zeros_like(partial_value)
        momentum = BETA * momentum + partial_value
        col_width = partial_value.shape[2]
        own_cols = lax.dynamic_slice_in_dim(
            weights, lax.axis_index("seq") * col_width, col_width, 2
        )
        updated = own_cols - step_scale * normalize_columns(momentum)
        weights = lax.all_gather(updated.astype(jnp.bfloat16), "seq", axis=2, tiled=True).astype(
            updated.dtype
        )
        outputs.append(apply_fast(weights, queries))
    return jnp.stack(outputs).astype(jnp.bfloat16)


def solution(mesh):
    in_specs = (
        P(None, None, ("seq", "wide"), None),
        P(),
        P(None, "wide", None),
        P(None, "wide", None, None),
        P("wide"),
    )
    out_specs = P(None, "seq", "wide")
    return jax.shard_map(local, mesh=mesh, in_specs=in_specs, out_specs=out_specs, check_vma=False)
```

profile of v0, /device:TPU:1, one launch (start us, length us, event | category | flops | bytes accessed | tf_op | source)
XLA Modules:
  0.0 391.9 jit_solution(1343971738967187830)
XLA Ops:
  6.5 1.3 slice.104
  7.9 3.9 collective-permute-start
  11.8 2.1 fusion.88
  14.1 15.5 %collective-permute-done = bf16[3,2,3,8192]{3,2,1,0:T(4,128)(2,1)S(1)} collective-permute-done((bf16[3,2,3,8192]{3,2,1,0:T(4,128)(2,1)S(1)}, bf16[3,2,3,8192]{3,2,1,0:T(4,128)(2,1)S(1)}, u32[]{:S(2)}, u32[]{:S(2)}) %collective-permute-start) | collective-permute-done | bytes 294944 | tf_op jit(solution)/shard_map/ppermute | solution.py:18
  30.0 14.6 %multiply_convert_fusion = bf16[3,2,64,8192]{3,2,1,0:T(8,128)(2,1)S(1)} fusion(bf16[3,2,64,8192]{3,2,1,0:T(8,128)(2,1)} %param.5, bf16[3,2,3,8192]{3,2,1,0:T(4,128)(2,1)S(1)} %pad_select_fusion, f32[3,8192]{1,0:T(4,128)S(1)} %get-tuple-element.25, f32[3,8192]{1,0:T(4,128)S(1)} %get-tuple-element.26, f32[3,8192]{1,0:T(4,128)S(1)} %get-tuple-element.27, ...), kind=kLoop, calls=%fused_computation | loop fusion | flops 78643200 | bytes 13271040 | tf_op jit(solution)/shard_map/convert_element_type | solution.py:126
  44.5 2.9 copy.73
  47.4 2.4 fusion.87
  49.8 3.4 copy.40
  53.3 10.9 %all-to-all-start.1 = ((bf16[16,3,2,32,512]{4,3,2,1,0:T(8,128)(2,1)}), bf16[16,3,2,32,512]{4,3,2,1,0:T(8,128)(2,1)S(1)}, u32[]{:S(2)}, u32[]{:S(2)}) async-start(bf16[16,3,2,32,512]{4,3,2,1,0:T(8,128)(2,1)} %copy.40), calls=%async_computation.1 | async-start | bytes 6291456 | tf_op jit(solution)/shard_map/all_to_all | solution.py:45
  64.2 5.3 %copy.39 = bf16[16,3,2,32,512]{4,3,2,1,0:T(8,128)(2,1)} copy(bf16[16,3,2,32,512]{4,0,3,2,1:T(8,128)(2,1)} %get-tuple-element.11) | data formatting | bytes 6291456 | tf_op jit(solution)/shard_map/split | solution.py:43
  69.5 69.8 %all-to-all-done.1 = bf16[16,3,2,32,512]{4,3,2,1,0:T(8,128)(2,1)S(1)} async-done(((bf16[16,3,2,32,512]{4,3,2,1,0:T(8,128)(2,1)}), bf16[16,3,2,32,512]{4,3,2,1,0:T(8,128)(2,1)S(1)}, u32[]{:S(2)}, u32[]{:S(2)}) %all-to-all-start.1) | async-done | bytes 3145760 | tf_op jit(solution)/shard_map/all_to_all | solution.py:45
  139.3 5.7 %all-to-all-start = ((bf16[16,3,2,32,512]{4,3,2,1,0:T(8,128)(2,1)}), bf16[16,3,2,32,512]{4,3,2,1,0:T(8,128)(2,1)}, u32[]{:S(2)}, u32[]{:S(2)}) async-start(bf16[16,3,2,32,512]{4,3,2,1,0:T(8,128)(2,1)} %copy.39), calls=%async_computation | async-start | bytes 6291456 | tf_op jit(solution)/shard_map/all_to_all | solution.py:45
  145.0 3.2 convert_element_type.142
  148.3 68.8 %all-to-all-done = bf16[16,3,2,32,512]{4,3,2,1,0:T(8,128)(2,1)} async-done(((bf16[16,3,2,32,512]{4,3,2,1,0:T(8,128)(2,1)}), bf16[16,3,2,32,512]{4,3,2,1,0:T(8,128)(2,1)}, u32[]{:S(2)}, u32[]{:S(2)}) %all-to-all-start) | async-done | bytes 3145760 | tf_op jit(solution)/shard_map/all_to_all | solution.py:45
  217.1 2.5 pad_maximum_fusion.1
  219.6 0.8 copy.64
  220.6 2.4 copy-done
  223.0 0.9 fusion.2
  223.9 1.3 copy.44
  225.2 2.3 fusion.54
  227.5 2.3 fusion.58
  229.8 2.7 fusion.28
  232.5 0.8 fusion.37
  233.4 0.8 fusion.36
  234.2 0.4 copy-done.2
  234.6 0.8 fusion.34
  235.6 1.2 copy.46
  236.9 5.8 %all-to-all-start.2 = ((bf16[16,3,512,32]{2,3,1,0:T(8,128)(2,1)}), bf16[16,3,512,32]{2,3,1,0:T(8,128)(2,1)S(1)}, u32[]{:S(2)}, u32[]{:S(2)}) async-start(bf16[16,3,512,32]{2,3,1,0:T(8,128)(2,1)} %copy.46), calls=%async_computation.2 | async-start | bytes 3145728 | tf_op jit(solution)/shard_map/all_to_all | solution.py:51
  242.7 2.3 constant_dynamic-slice_fusion
  245.0 1.4 copy.43
  247.0 17.0 %all-to-all-done.2 = bf16[16,3,512,32]{2,3,1,0:T(8,128)(2,1)S(1)} async-done(((bf16[16,3,512,32]{2,3,1,0:T(8,128)(2,1)}), bf16[16,3,512,32]{2,3,1,0:T(8,128)(2,1)S(1)}, u32[]{:S(2)}, u32[]{:S(2)}) %all-to-all-start.2) | async-done | bytes 1572896 | tf_op jit(solution)/shard_map/all_to_all | solution.py:51
  264.4 0.7 fusion.66
  265.5 0.5 copy.51
  266.0 36.2 %all-gather.3.cloned.1.call-done = bf16[3,512,512]{1,2,0:T(8,128)(2,1)} async-done(((bf16[3,512,32]{1,2,0:T(8,128)(2,1)}), bf16[3,512,512]{1,2,0:T(8,128)(2,1)}) %all-gather.3.cloned.1.call-update) | async-done | bytes 1572880 | tf_op jit(solution)/shard_map/all_gather | solution.py:150
  302.2 2.3 fusion.45
  304.5 2.1 fusion.49
  306.5 3.3 fusion.19
  309.8 2.0 fusion.39
  311.9 2.0 fusion.38
  313.9 0.9 fusion.35
  315.1 25.0 %all_to_all.20 = bf16[16,3,512,32]{2,3,1,0:T(8,128)(2,1)S(1)} all-to-all(bf16[16,3,512,32]{2,3,1,0:T(8,128)(2,1)S(1)} %copy.53), channel_id=1, replica_groups=mesh['seq'=16,'wide'=16] {'seq'}, dimensions={0} | all-to-all | bytes 3145728 | tf_op jit(solution)/shard_map/all_to_all | solution.py:51
  340.5 0.7 subtract_convert_fusion
  341.3 3.4 fusion.65
  344.7 3.4 fusion.32
  348.1 28.3 %all-gather.5.cloned.1.call-done = bf16[3,512,512]{1,2,0:T(8,128)(2,1)} async-done(((bf16[3,512,32]{1,2,0:T(8,128)(2,1)}), bf16[3,512,512]{1,2,0:T(8,128)(2,1)}) %all-gather.5.cloned.1.call-update) | async-done | bytes 1572880 | tf_op jit(solution)/shard_map/all_gather | solution.py:150
  376.4 3.5 fusion.62
  379.9 3.6 fusion.33
  383.5 1.5 pad_maximum_fusion.2
  (31 shorter events, 2.4 us)
Async XLA Ops:
  7.9 21.8 %collective-permute-start = (bf16[3,2,3,8192]{3,2,1,0:T(4,128)(2,1)S(1)}, bf16[3,2,3,8192]{3,2,1,0:T(4,128)(2,1)S(1)}, u32[]{:S(2)}, u32[]{:S(2)}) collective-permute-start(bf16[3,2,3,8192]{3,2,1,0:T(4,128)(2,1)S(1)} %slice.104), channel_id=1, source_target_pairs={{0,1},{1,2},{2,3},{3,4},{4,5},{5,6},{6,7},{7,8},{8,9},{9,10},{10,1... | collective-permute-start | bytes 884744 | tf_op jit(solution)/shard_map/ppermute | solution.py:18
  53.3 86.0 %all-to-all-start.1 = ((bf16[16,3,2,32,512]{4,3,2,1,0:T(8,128)(2,1)}), bf16[16,3,2,32,512]{4,3,2,1,0:T(8,128)(2,1)S(1)}, u32[]{:S(2)}, u32[]{:S(2)}) async-start(bf16[16,3,2,32,512]{4,3,2,1,0:T(8,128)(2,1)} %copy.40), calls=%async_computation.1 | async-start | bytes 6291456 | tf_op jit(solution)/shard_map/all_to_all | solution.py:45
  139.3 77.7 %all-to-all-start = ((bf16[16,3,2,32,512]{4,3,2,1,0:T(8,128)(2,1)}), bf16[16,3,2,32,512]{4,3,2,1,0:T(8,128)(2,1)}, u32[]{:S(2)}, u32[]{:S(2)}) async-start(bf16[16,3,2,32,512]{4,3,2,1,0:T(8,128)(2,1)} %copy.39), calls=%async_computation | async-start | bytes 6291456 | tf_op jit(solution)/shard_map/all_to_all | solution.py:45
  145.0 3.3 copy-start.4
  220.4 2.6 copy-start
  225.2 4.5 %copy-start.1 = (bf16[16,3,2,64,512]{4,3,0,2,1:T(8,128)(2,1)S(1)}, bf16[16,3,2,64,512]{4,3,0,2,1:T(8,128)(2,1)}, u32[]{:S(2)}) copy-start(bf16[16,3,2,64,512]{4,3,0,2,1:T(8,128)(2,1)} %copy-done) | copy-start | bytes 18874372
  233.4 1.2 copy-start.2
  236.9 27.2 %all-to-all-start.2 = ((bf16[16,3,512,32]{2,3,1,0:T(8,128)(2,1)}), bf16[16,3,512,32]{2,3,1,0:T(8,128)(2,1)S(1)}, u32[]{:S(2)}, u32[]{:S(2)}) async-start(bf16[16,3,512,32]{2,3,1,0:T(8,128)(2,1)} %copy.46), calls=%async_computation.2 | async-start | bytes 3145728 | tf_op jit(solution)/shard_map/all_to_all | solution.py:51
  242.7 59.5 %all-gather.3.cloned.1.call-start = ((), (), s32[]{:S(2)}) async-start(), calls=%async_computation.4 | async-start | bytes 1671168 | tf_op jit(solution)/shard_map/all_gather | solution.py:150
  265.2 111.2 %all-gather.5.cloned.1.call-start = ((), (), s32[]{:S(2)}) async-start(), calls=%async_computation.5 | async-start | bytes 1671168 | tf_op jit(solution)/shard_map/all_gather | solution.py:150
  302.2 2.3 copy-start.3
Sparse Core Ops, SparseCore 0:
  265.3 36.8 all-gather.2
  341.4 34.9 all-gather.4
where the time goes:
time: 393 us; the launch traced here: 392 us
  waiting for transfers between devices  236 us (60%)
  matrix products  36.2 us (9%)
  local copies, waits for them, and re-layouts  28.3 us (7%)
  starting transfers between devices  26.6 us (7%)
  other arithmetic  25.8 us (7%)
  blocking collectives  25 us (6%)
  between operations  14.4 us (4%)
    all_to_all x2, waiting for transfers between devices, several_exchanges(): lax.all_to_all(slab, axis, split_axis=0, concat_axis=0, tiled=True)  139 us
    all_gather x2, waiting for transfers between devices, local(): lax.all_gather(updated.astype(jnp.bfloat16), 'seq', axis=2, tiled=True)  64.5 us
    all_to_all x1, blocking collectives, summed_on_arrival(): lax.all_to_all(cut_along(value, dim, devices), axis, 0, 0, tiled=True)  25 us
    dot_general x8, matrix products, matmul(): return jnp.dot(left, right, preferred_element_type=jnp.float32)  24.2 us
    all_to_all x1, waiting for transfers between devices, summed_on_arrival(): lax.all_to_all(cut_along(value, dim, devices), axis, 0, 0, tiled=True)  17 us
    all_to_all x2, starting transfers between devices, several_exchanges(): lax.all_to_all(slab, axis, split_axis=0, concat_axis=0, tiled=True)  16.6 us
    ppermute x1, waiting for transfers between devices, from_behind(): return lax.ppermute(value, axis, pairs)  15.5 us
    convert_element_type x1, other arithmetic, local(): jax.nn.silu(conv_rows(extended, conv_kernel, row_count))  14.6 us
  transfers between devices with their start and end apart: 6, of which 6 were waited for; matrix products, arithmetic and copies ran while one was open for 6% of the time, Pallas kernels for 0%

commit v1 on v0

v1 whole, which is shorter than its diff:
```python
import jax
import jax.numpy as jnp
from jax import lax
from jax.experimental import pallas as pl
from jax.experimental.pallas import tpu as pltpu
from jax.sharding import PartitionSpec as P


HEAD = 512
GROUPS = 2
KW = 4
EPS = 1e-06
BETA = 0.6
ROWS = 1024
CHUNK = 256
BLOCKS = ROWS // CHUNK
LEAD = CHUNK // 64
BF = jnp.bfloat16
F32 = jnp.float32


def vmem():
    return pl.BlockSpec(memory_space=pltpu.VMEM)


def anywhere():
    return pl.BlockSpec(memory_space=pl.ANY)


def call(body, outs, ins, scratch=(), flops=0, nbytes=1 << 18, out_specs=None, limit=16, **more):
    return pl.pallas_call(
        body,
        out_shape=outs,
        in_specs=ins,
        out_specs=jax.tree.map(lambda _: vmem(), outs) if out_specs is None else out_specs,
        scratch_shapes=list(scratch),
        cost_estimate=pl.CostEstimate(flops=flops, bytes_accessed=nbytes, transcendentals=0),
        compiler_params=pltpu.CompilerParams(vmem_limit_bytes=limit << 20),
        **more,
    )


def sds(shape, dtype):
    return jax.ShapeDtypeStruct(shape, dtype)


def sigmoid(x):
    return 0.5 * jnp.tanh(0.5 * x) + 0.5


def conv_silu(current, previous, taps):
    extended = jnp.concatenate([previous, current], axis=0)
    total = taps[0:1] * current
    for j in range(1, KW):
        total = total + taps[j : j + 1] * pltpu.roll(extended, j, 0)[8:]
    return (total * sigmoid(total)).astype(BF)


def rms_scaled(act, gain):
    wide = act.astype(F32)
    scale = lax.rsqrt(jnp.mean(wide * wide, axis=-1, keepdims=True) + EPS)
    return (wide * scale * gain).astype(BF)


def nt(left, right):
    return lax.dot_general(left, right, (((1,), (1,)), ((), ())), preferred_element_type=F32)


def nn(left, right):
    return jnp.dot(left, right, preferred_element_type=F32)


def tn(left, right):
    return lax.dot_general(left, right, (((0,), (0,)), ((), ())), preferred_element_type=F32)


def own_taps(taps, stream):
    cols = pl.ds(pl.multiple_of(lax.axis_index("wide") * HEAD, HEAD), HEAD)
    return taps[stream, :, cols]


def edge_rows(first, tails, earlier, stream):
    later = lax.axis_index("seq") > 0
    here = tails[stream].astype(F32)
    if first:
        return jnp.where(later, here, jnp.zeros_like(here))
    return jnp.where(later, here, earlier[stream].astype(F32))


def conv_chunk(raw, stream, n, edge, taps):
    current = raw[pl.ds(LEAD * n, LEAD), stream].reshape(CHUNK, HEAD).astype(F32)
    inner = raw[jnp.maximum(LEAD * n - 1, 0), stream, 48:64, :].astype(F32)[8:]
    return conv_silu(current, jnp.where(n == 0, edge, inner), taps)


def chunk_rows(n):
    return pl.ds(pl.multiple_of(n * CHUNK, CHUNK), CHUNK)


def hbm():
    return pl.BlockSpec(memory_space=pltpu.HBM)


def spread_of(first_stream, streams, group):
    def body(source, out, stage, sems_in, sems_out):
        def pull(s, h):
            cols = pl.ds(h * HEAD, HEAD)
            spot = source.at[first_stream + s, group, :, cols]
            return pltpu.make_async_copy(spot, stage.at[s, h], sems_in.at[s, h])

        def push(s, h):
            return pltpu.make_async_copy(stage.at[s, h], out.at[h, s], sems_out.at[s, h])

        spots = [(s, h) for s in range(streams) for h in range(16)]
        for spot in spots:
            pull(*spot).start()
        for spot in spots:
            pull(*spot).wait()
            push(*spot).start()
        for spot in spots:
            push(*spot).wait()

    return call(
        body,
        sds((16, streams, 64, HEAD), BF),
        [hbm()],
        [
            pltpu.VMEM((streams, 16, 64, HEAD), BF),
            pltpu.SemaphoreType.DMA((streams, 16)),
            pltpu.SemaphoreType.DMA((streams, 16)),
        ],
        nbytes=streams << 21,
        out_specs=hbm(),
    )


def prepare(first, raw, tails, earlier, taps, gain):
    def body(raw, tails, earlier, taps, gain, keys, values):
        key_taps, value_taps = own_taps(taps, 1), own_taps(taps, 2)
        key_edge = edge_rows(first, tails, earlier, 0)
        value_edge = edge_rows(first, tails, earlier, 1)

        def step(n, carry):
            rows = chunk_rows(n)
            keys[rows, :] = rms_scaled(conv_chunk(raw, 0, n, key_edge, key_taps), gain[1])
            act = conv_chunk(raw, 1, n, value_edge, value_taps)
            values[rows, :] = (act.astype(F32) * (-1.0 / 16384)).astype(BF)
            return carry

        lax.fori_loop(0, BLOCKS, step, 0)

    rows = sds((ROWS, HEAD), BF)
    return call(body, [rows, rows], [vmem()] * 5, nbytes=8 << 20)(raw, tails, earlier, taps, gain)


def prepare_queries(first, raw, tails, earlier, taps, gain):
    def body(raw, tails, earlier, taps, gain, queries):
        query_taps = own_taps(taps, 0)
        edge = edge_rows(first, tails, earlier, 0)

        def step(n, carry):
            queries[chunk_rows(n), :] = rms_scaled(conv_chunk(raw, 0, n, edge, query_taps), gain[0])
            return carry

        lax.fori_loop(0, BLOCKS, step, 0)

    return call(body, sds((ROWS, HEAD), BF), [vmem()] * 5, nbytes=4 << 20)(
        raw, tails, earlier, taps, gain
    )


def gradients(keys, values, weights, plain):
    def body(keys, values, weights, keep, send, hs, gs, us):
        core = lax.axis_index("seq") & 1
        wg, wu, wd = (weights[m].astype(BF) for m in range(3))

        def step(n, carry):
            rows = chunk_rows(n)
            k = keys[rows, :]
            v = values[rows, :]
            if plain:
                a, b, back = nn(k, wg), nn(k, wu), nt(v, wd)
            else:
                a, b, back = nt(k, wg), nt(k, wu), nn(v, wd)
            sg = sigmoid(a)
            act = a * sg
            hs[rows, :] = (act * b).astype(BF)
            gs[rows, :] = (back * b * sg * (1.0 + a * (1.0 - sg))).astype(BF)
            us[rows, :] = (back * act).astype(BF)
            return carry

        lax.fori_loop(0, BLOCKS, step, 0)
        for half, out in ((1, send), (0, keep)):
            side = jnp.bitwise_xor(core, half)

            def block(n, carry, out=out, side=side):
                cols = pl.ds(pl.multiple_of(side * 256 + n * 128, 128), 128)
                for m, (left, right) in enumerate(((gs, keys), (us, keys), (values, hs))):
                    part = tn(left[:, cols], right[...]).astype(BF)
                    for q in range(2):
                        out[2 * n + q, m] = part[64 * q : 64 * q + 64]
                return carry

            lax.fori_loop(0, 2, block, 0)

    half = sds((4, 3, 64, HEAD), BF)
    return call(
        body,
        [half, half],
        [vmem()] * 3,
        [pltpu.VMEM((ROWS, HEAD), BF)] * 3,
        flops=6 * 2 * ROWS * HEAD * HEAD,
        nbytes=4 << 20,
        limit=24,
    )(keys, values, weights)


def pair_sum(keep, recv):
    def body(keep, recv, own, *sends):
        y = lax.axis_index("seq") >> 1 & 3
        own[...] = keep[y].astype(F32) + recv[y].astype(F32)
        for d, out in enumerate(sends):
            other = y + (d + 1) & 3
            out[...] = (keep[other].astype(F32) + recv[other].astype(F32)).astype(BF)

    block = (3, 64, HEAD)
    return call(body, [sds(block, F32)] + [sds(block, BF)] * 3, [vmem()] * 2)(keep, recv)


def ring_sum(own, parts):
    def body(own, one, two, three, out):
        out[...] = (own[...] + one[...].astype(F32) + two[...].astype(F32) + three[...].astype(F32)).astype(BF)

    return call(body, sds((3, 64, HEAD), BF), [vmem()] * 4)(own, *parts)


def update(scale, mine, recv, weights, moment):
    fresh = moment is None

    def body(scale, mine, recv, weights, *rest):
        grad = mine[...].astype(F32) + recv[...].astype(F32)
        if fresh:
            mom = grad
        else:
            mom = BETA * rest[0][...] + grad
        moment_out, weights_out, narrow = rest[-3:]
        norm = lax.rsqrt(jnp.mean(mom * mom, axis=-1, keepdims=True) + EPS)
        new = weights[...] - (scale[0] * HEAD ** (-0.5)) * (mom * norm)
        moment_out[...] = mom
        weights_out[...] = new
        narrow[...] = new.astype(BF)

    block = (3, 64, HEAD)
    ins = [scale, mine, recv, weights] + ([] if fresh else [moment])
    return call(
        body,
        [sds(block, F32), sds(block, F32), sds(block, BF)],
        [pl.BlockSpec(memory_space=pltpu.SMEM)] + [vmem()] * (len(ins) - 1),
    )(*ins)


def assemble(pieces):
    def body(*refs):
        out = refs[8]
        seq = lax.axis_index("seq")
        core, y = seq & 1, seq >> 1 & 3
        for k, piece in enumerate(refs[:8]):
            side = jnp.bitwise_xor(core, k // 4)
            spot = y + 4 - k % 4 & 3
            rows = pl.ds(pl.multiple_of(side * 256 + spot * 64, 64), 64)
            for m in range(3):
                out[m, rows, :] = piece[m]

    return call(body, sds((3, HEAD, HEAD), BF), [vmem()] * 8)(*pieces)


def apply_fast(queries, weights, group, earlier):
    def body(queries, weights, *rest):
        out, stage, sems = rest[-3:]

        def copy(n):
            rows = chunk_rows(n)
            return pltpu.make_async_copy(stage.at[rows], out.at[group, rows], sems.at[n])

        def step(n, carry):
            rows = chunk_rows(n)
            q = queries[rows, :]
            a = nt(q, weights[0])
            b = nt(q, weights[1])
            hidden = (a * sigmoid(a) * b).astype(BF)
            stage[rows, :] = nt(hidden, weights[2]).astype(BF)
            copy(n).start()
            return carry

        lax.fori_loop(0, BLOCKS, step, 0)
        for n in range(BLOCKS):
            copy(n).wait()

    more = [] if earlier is None else [earlier]
    return call(
        body,
        sds((GROUPS, ROWS, HEAD), BF),
        [vmem()] * 2 + [anywhere()] * len(more),
        [pltpu.VMEM((ROWS, HEAD), BF), pltpu.SemaphoreType.DMA((BLOCKS,))],
        flops=3 * 2 * ROWS * HEAD * HEAD,
        nbytes=4 << 20,
        out_specs=anywhere(),
        input_output_aliases={2: 0} if more else {},
    )(queries, weights, *more)


def seq_permute(value, target):
    return lax.ppermute(value, "seq", [(i, target(i)) for i in range(16)])


def core_swap(value):
    return seq_permute(value, lambda i: i ^ 1)


def z_swap(value):
    return seq_permute(value, lambda i: i ^ 8)


def y_shift(value, d):
    return seq_permute(value, lambda i: (i & 9) | (((i >> 1 & 3) + d & 3) << 1))


def regroup(qkv_proj, first_stream, streams, group):
    spread = spread_of(first_stream, streams, group)(qkv_proj)
    return lax.all_to_all(spread, "wide", 0, 0, tiled=True)


def tails_behind(raw):
    return seq_permute(raw[15, :, 56:64, :], lambda i: (i + 1) % 16)


def reduce_pieces(keep, send):
    recv = core_swap(send)
    own, *sends = pair_sum(keep, recv)
    parts = [y_shift(s, d + 1) for d, s in enumerate(sends)]
    mine = ring_sum(own, parts)
    return mine, z_swap(mine)


def gather_pieces(narrow):
    pieces = [narrow] + [y_shift(narrow, d) for d in (1, 2, 3)]
    return pieces + [core_swap(p) for p in pieces]


def local(qkv_proj, conv_kernel, qk_gain, fast_init, step_size):
    return program(qkv_proj, conv_kernel, qk_gain, fast_init[:, 0], step_size)


def program(qkv_proj, conv_kernel, qk_gain, start, step_size):
    seq = lax.axis_index("seq")
    own_at = (seq & 1) * 256 + (seq >> 1 & 3) * 64
    state = jnp.swapaxes(lax.dynamic_slice_in_dim(start, own_at, 64, 2), 1, 2)

    kv0 = regroup(qkv_proj, 1, 2, 0)
    tails0 = tails_behind(kv0)
    kv1 = regroup(qkv_proj, 1, 2, 1)
    tails1 = tails_behind(kv1)
    q0 = regroup(qkv_proj, 0, 1, 0)
    qtails0 = tails_behind(q0)
    q1 = regroup(qkv_proj, 0, 1, 1)
    qtails1 = tails_behind(q1)

    keys, values = prepare(True, kv0, tails0, tails0, conv_kernel, qk_gain)
    mine, recv = reduce_pieces(*gradients(keys, values, start, True))
    moment, state, narrow = update(step_size, mine, recv, state, None)
    weights1 = assemble(gather_pieces(narrow))
    keys, values = prepare(False, kv1, tails1, tails0, conv_kernel, qk_gain)
    mine, recv = reduce_pieces(*gradients(keys, values, weights1, False))
    moment, state, narrow = update(step_size, mine, recv, state, moment)
    weights2 = assemble(gather_pieces(narrow))
    queries0 = prepare_queries(True, q0, qtails0, qtails0, conv_kernel, qk_gain)
    out = apply_fast(queries0, weights1, 0, None)
    queries1 = prepare_queries(False, q1, qtails1, qtails0, conv_kernel, qk_gain)
    return apply_fast(queries1, weights2, 1, out)


def solution(mesh):
    in_specs = (
        P(None, None, ("seq", "wide"), None),
        P(),
        P(None, "wide", None),
        P(None, "wide", None, None),
        P("wide"),
    )
    out_specs = P(None, "seq", "wide")
    return jax.shard_map(local, mesh=mesh, in_specs=in_specs, out_specs=out_specs, check_vma=False)
```

time: 393 us -> 300 us (0.76)
  waiting for transfers between devices: 236 us -> 81.4 us
  starting transfers between devices: 26.6 us -> 134 us
  Pallas kernels: 0 us -> 49 us
  matrix products: 36.2 us -> 0 us
  other arithmetic: 25.8 us -> 0 us
  blocking collectives: 25 us -> 0 us
  between operations: 14.4 us -> 1.18 us
    all_to_all x3 -> x4, waiting for transfers between devices: 156 us -> 50.9 us  [regroup(): return lax.all_to_all(spread, 'wide', 0, 0, tiled=True)]
    ppermute x1 -> x28, starting transfers between devices: 3.89 us -> 94.5 us  [seq_permute(): return lax.ppermute(value, 'seq', [(i, target(i)) for i in range(16)])]
    all_gather x2 -> x0, waiting for transfers between devices: 64.5 us -> none  [local(): lax.all_gather(updated.astype(jnp.bfloat16), 'seq', axis=2, tiled=True)]
    pallas_call x0 -> x20, Pallas kernels: none -> 49 us  [the longest x2 10.8 us: gradients(): call(body, [half, half], [vmem()] * 3, [pltpu.VMEM((ROWS, HEAD), BF)] * 3...]
    dot_general x16 -> x0, matrix products: 36.2 us -> none  [the longest x8 24.2 us: matmul(): return jnp.dot(left, right, preferred_element_type=jnp.float32)]
    all_to_all x1 -> x0, blocking collectives: 25 us -> none  [summed_on_arrival(): lax.all_to_all(cut_along(value, dim, devices), axis, 0, 0, tiled=True)]
    convert_element_type x4 -> x0, other arithmetic: 19.3 us -> none  [the longest x1 14.6 us: local(): jax.nn.silu(conv_rows(extended, conv_kernel, row_count))]
    unnamed x13 -> x38, local copies, waits for them, and re-layouts: 6.04 us -> 23.5 us
  transfers between devices with their start and end apart: 6 -> 32, of which waited for: 6 -> 12; matrix products, arithmetic and copies ran while one was open for 6% -> 2% of each run, Pallas kernels for 0% -> 14%
where the time goes in v1:
time: 300 us; the launch traced here: 295 us
  starting transfers between devices  134 us (45%)
  waiting for transfers between devices  81.4 us (27%)
  Pallas kernels  49 us (16%)
  local copies, waits for them, and re-layouts  29.4 us (10%)
    ppermute x28, starting transfers between devices, seq_permute(): return lax.ppermute(value, 'seq', [(i, target(i)) for i in range(16)])  94.5 us
    all_to_all x4, waiting for transfers between devices, regroup(): return lax.all_to_all(spread, 'wide', 0, 0, tiled=True)  50.9 us
    all_to_all x4, starting transfers between devices, regroup(): return lax.all_to_all(spread, 'wide', 0, 0, tiled=True)  39.7 us
    ppermute x28, waiting for transfers between devices, seq_permute(): return lax.ppermute(value, 'seq', [(i, target(i)) for i in range(16)])  30.5 us
    unnamed x38, local copies, waits for them, and re-layouts  23.5 us
    pallas_call x2, Pallas kernels, gradients(): call(body, [half, half], [vmem()] * 3, [pltpu.VMEM((ROWS, HEAD), BF)] * 3...  10.8 us
    pallas_call x4, Pallas kernels, regroup(): spread = spread_of(first_stream, streams, group)(qkv_proj)  10.7 us
    pallas_call x2, Pallas kernels, prepare(): call(body, [rows, rows], [vmem()] * 5, nbytes=8 << 20)  8.58 us
  transfers between devices with their start and end apart: 32, of which 12 were waited for; matrix products, arithmetic and copies ran while one was open for 2% of the time, Pallas kernels for 14%

profile of v1, /device:TPU:1, one launch (start us, length us, event | category | flops | bytes accessed | tf_op | source)
XLA Modules:
  0.0 295.1 jit_solution(3701944509202994356)
XLA Ops:
  0.0 2.8 copy-done
  4.2 11.6 %all-to-all-start.1 = ((bf16[16,1,64,512]{3,2,1,0:T(8,128)(2,1)}), bf16[16,1,64,512]{3,2,1,0:T(8,128)(2,1)S(1)}, u32[]{:S(2)}, u32[]{:S(2)}) async-start(bf16[16,1,64,512]{3,2,1,0:T(8,128)(2,1)} %shard_map.56), calls=%async_computation.1 | async-start | bytes 2097152 | tf_op jit(solution)/shard_map/all_to_all | solution.py:330
  15.8 2.8 copy-done.1
  18.6 3.7 %shard_map.59 = bf16[16,2,64,512]{3,2,1,0:T(8,128)(2,1)S(1)} custom-call(bf16[3,2,64,8192]{3,2,1,0:T(8,128)(2,1)S(1)} %copy-done.1), custom_call_target="tpu_custom_call" | custom-call | bytes 4194304 | tf_op jit(solution)/shard_map/pallas_call | solution.py:329
  23.7 18.2 %all-to-all-done.1.raw = bf16[16,1,64,512]{3,2,1,0:T(8,128)(2,1)S(1)} async-done(((bf16[16,1,64,512]{3,2,1,0:T(8,128)(2,1)}), bf16[16,1,64,512]{3,2,1,0:T(8,128)(2,1)S(1)}, u32[]{:S(2)}, u32[]{:S(2)}) %all-to-all-start.1) | async-done | bytes 1048608 | tf_op jit(solution)/shard_map/all_to_all | solution.py:330
  41.9 6.6 %all-to-all-start.3 = ((bf16[16,2,64,512]{3,2,1,0:T(8,128)(2,1)}), bf16[16,2,64,512]{3,2,1,0:T(8,128)(2,1)S(1)}, u32[]{:S(2)}, u32[]{:S(2)}) async-start(bf16[16,2,64,512]{3,2,1,0:T(8,128)(2,1)} %copy-done.7), calls=%async_computation.3 | async-start | bytes 4194304 | tf_op jit(solution)/shard_map/all_to_all | solution.py:330
  48.5 2.8 copy-done.2
  51.3 3.7 %shard_map.58 = bf16[16,2,64,512]{3,2,1,0:T(8,128)(2,1)S(1)} custom-call(bf16[3,2,64,8192]{3,2,1,0:T(8,128)(2,1)S(1)} %copy-done.2), custom_call_target="tpu_custom_call" | custom-call | bytes 4194304 | tf_op jit(solution)/shard_map/pallas_call | solution.py:329
  56.4 32.6 %all-to-all-done.3.raw = bf16[16,2,64,512]{3,2,1,0:T(8,128)(2,1)S(1)} async-done(((bf16[16,2,64,512]{3,2,1,0:T(8,128)(2,1)}), bf16[16,2,64,512]{3,2,1,0:T(8,128)(2,1)S(1)}, u32[]{:S(2)}, u32[]{:S(2)}) %all-to-all-start.3) | async-done | bytes 2097184 | tf_op jit(solution)/shard_map/all_to_all | solution.py:330
  90.4 14.1 %all-to-all-start.2 = ((bf16[16,2,64,512]{3,2,1,0:T(8,128)(2,1)}), bf16[16,2,64,512]{3,2,1,0:T(8,128)(2,1)S(1)}, u32[]{:S(2)}, u32[]{:S(2)}) async-start(bf16[16,2,64,512]{3,2,1,0:T(8,128)(2,1)} %copy-done.6), calls=%async_computation.2 | async-start | bytes 4194304 | tf_op jit(solution)/shard_map/all_to_all | solution.py:330
  105.2 4.7 %collective-permute-start.3 = (bf16[2,8,512]{2,1,0:T(8,128)(2,1)S(1)}, bf16[2,8,512]{2,1,0:T(8,128)(2,1)S(1)}, u32[]{:S(2)}, u32[]{:S(2)}) collective-permute-start(bf16[2,8,512]{2,1,0:T(8,128)(2,1)S(1)} %slice_bitcast_fusion), channel_id=1, source_target_pairs={{0,16},{16,32},{32,48},{48,64},{64,80},{80,96},{96,112},{112,128},... | collective-permute-start | bytes 49160 | tf_op jit(solution)/shard_map/ppermute | solution.py:313
  110.8 1.6 copy-done.5
  113.0 4.3 %shard_map.61 = (bf16[1024,512]{1,0:T(8,128)(2,1)S(1)}, bf16[1024,512]{1,0:T(8,128)(2,1)S(1)}) custom-call(bf16[16,2,64,512]{3,2,1,0:T(8,128)(2,1)S(1)} %copy-done.5, bf16[2,8,512]{2,1,0:T(8,128)(2,1)S(1)} %collective-permute-done.3.earlier.tails, bf16[2,8,512]{2,1,0:T(8,128)(2,1)S(1)} %collective-permute-done.3.earlier.tails, f32[3,4,8192]{2,1,0:T(4,128)S(1)} %copy-done.8, ...), custom_call_target="tpu_custom_call" | custom-call | bytes 8388608 | tf_op jit(solution)/shard_map/pallas_call | solution.py:153
  117.4 1.9 copy-done.15
  119.2 5.2 %shard_map.62 = (bf16[4,3,64,512]{3,2,1,0:T(8,128)(2,1)S(1)}, bf16[4,3,64,512]{3,2,1,0:T(8,128)(2,1)S(1)}) custom-call(bf16[1024,512]{1,0:T(8,128)(2,1)S(1)} %get-tuple-element.27.keys, bf16[1024,512]{1,0:T(8,128)(2,1)S(1)} %get-tuple-element.28.values, f32[3,512,512]{2,1,0:T(8,128)S(1)} %bitcast.13), custom_call_target="tpu_custom_call" | custom-call | flops 3221225472 | bytes 4194304 | tf_op jit(solution)/shard_map/pallas_call | solution.py:207
  124.4 45.5 %collective-permute-start.4 = (bf16[4,3,64,512]{3,2,1,0:T(8,128)(2,1)S(1)}, bf16[4,3,64,512]{3,2,1,0:T(8,128)(2,1)S(1)}, u32[]{:S(2)}, u32[]{:S(2)}) collective-permute-start(bf16[4,3,64,512]{3,2,1,0:T(8,128)(2,1)S(1)} %get-tuple-element.30), channel_id=1, source_target_pairs={{0,16},{16,0},{32,48},{48,32},{64,80},{80,64},{96,112},{112,96},{1... | collective-permute-start | bytes 2359304 | tf_op jit(solution)/shard_map/ppermute | solution.py:313
  170.0 1.9 collective-permute-done.4.recv
  172.3 2.6 collective-permute-start.7
  174.8 9.2 %collective-permute-done.5.one = bf16[3,64,512]{2,1,0:T(8,128)(2,1)S(1)} collective-permute-done((bf16[3,64,512]{2,1,0:T(8,128)(2,1)S(1)}, bf16[3,64,512]{2,1,0:T(8,128)(2,1)S(1)}, u32[]{:S(2)}, u32[]{:S(2)}) %collective-permute-start.5) | collective-permute-done | bytes 196640 | tf_op jit(solution)/shard_map/ppermute | solution.py:313
  184.8 2.3 constant_dynamic-slice_fusion
  187.1 2.1 copy.7
  191.1 1.9 shard_map.65
  194.5 1.9 collective-permute-start.9
  196.4 2.7 collective-permute-start.10
  199.1 2.8 copy-done.3
  201.9 1.9 shard_map.55
  204.7 7.4 %all-to-all-start = ((bf16[16,1,64,512]{3,2,1,0:T(8,128)(2,1)}), bf16[16,1,64,512]{3,2,1,0:T(8,128)(2,1)}, u32[]{:S(2)}, u32[]{:S(2)}) async-start(bf16[16,1,64,512]{3,2,1,0:T(8,128)(2,1)} %copy-done.9), calls=%async_computation | async-start | bytes 2097152 | tf_op jit(solution)/shard_map/all_to_all | solution.py:330
  212.2 2.6 collective-permute-start.12
  215.4 2.0 collective-permute-start.2
  218.9 4.3 %shard_map.60 = (bf16[1024,512]{1,0:T(8,128)(2,1)S(1)}, bf16[1024,512]{1,0:T(8,128)(2,1)S(1)}) custom-call(bf16[16,2,64,512]{3,2,1,0:T(8,128)(2,1)S(1)} %all-to-all-done.2.raw, bf16[2,8,512]{2,1,0:T(8,128)(2,1)S(1)} %collective-permute-done.2.tails, bf16[2,8,512]{2,1,0:T(8,128)(2,1)S(1)} %collective-permute-done.3.earlier.tails, ...), custom_call_target="tpu_custom_call" | custom-call | bytes 8388608 | tf_op jit(solution)/shard_map/pallas_call | solution.py:153
  224.6 5.6 %shard_map.67 = (bf16[4,3,64,512]{3,2,1,0:T(8,128)(2,1)S(1)}, bf16[4,3,64,512]{3,2,1,0:T(8,128)(2,1)S(1)}) custom-call(bf16[1024,512]{1,0:T(8,128)(2,1)S(1)} %get-tuple-element.25.keys, bf16[1024,512]{1,0:T(8,128)(2,1)S(1)} %get-tuple-element.26.values, bf16[3,512,512]{2,1,0:T(8,128)(2,1)S(1)} %shard_map.66.weights), custom_call_target="tpu_custom_call" | custom-call | flops 3221225472 | bytes 4194304 | tf_op jit(solution)/shard_map/pallas_call | solution.py:207
  230.2 11.1 %collective-permute-start.16 = (bf16[4,3,64,512]{3,2,1,0:T(8,128)(2,1)S(1)}, bf16[4,3,64,512]{3,2,1,0:T(8,128)(2,1)S(1)}, u32[]{:S(2)}, u32[]{:S(2)}) collective-permute-start(bf16[4,3,64,512]{3,2,1,0:T(8,128)(2,1)S(1)} %get-tuple-element.37), channel_id=1, source_target_pairs={{0,16},{16,0},{32,48},{48,32},{64,80},{80,64},{96,112},{112,96},{1... | collective-permute-start | bytes 2359304 | tf_op jit(solution)/shard_map/ppermute | solution.py:313
  241.4 1.9 collective-permute-done.16.recv
  243.5 4.5 %collective-permute-start.18 = (bf16[3,64,512]{2,1,0:T(8,128)(2,1)S(1)}, bf16[3,64,512]{2,1,0:T(8,128)(2,1)S(1)}, u32[]{:S(2)}, u32[]{:S(2)}) collective-permute-start(bf16[3,64,512]{2,1,0:T(8,128)(2,1)S(1)} %get-tuple-element.40), channel_id=1, source_target_pairs={{0,64},{16,80},{32,96},{48,112},{64,0},{80,16},{96,32},{112,48},{1... | collective-permute-start | bytes 589832 | tf_op jit(solution)/shard_map/ppermute | solution.py:313
  248.1 4.0 %collective-permute-done.17.one = bf16[3,64,512]{2,1,0:T(8,128)(2,1)S(1)} collective-permute-done((bf16[3,64,512]{2,1,0:T(8,128)(2,1)S(1)}, bf16[3,64,512]{2,1,0:T(8,128)(2,1)S(1)}, u32[]{:S(2)}, u32[]{:S(2)}) %collective-permute-start.17) | collective-permute-done | bytes 196640 | tf_op jit(solution)/shard_map/ppermute | solution.py:313
  252.0 5.1 %collective-permute-done.18.two = bf16[3,64,512]{2,1,0:T(8,128)(2,1)S(1)} collective-permute-done((bf16[3,64,512]{2,1,0:T(8,128)(2,1)S(1)}, bf16[3,64,512]{2,1,0:T(8,128)(2,1)S(1)}, u32[]{:S(2)}, u32[]{:S(2)}) %collective-permute-start.18) | collective-permute-done | bytes 196640 | tf_op jit(solution)/shard_map/ppermute | solution.py:313
  257.2 3.7 %collective-permute-start.20 = (bf16[3,64,512]{2,1,0:T(8,128)(2,1)S(1)}, bf16[3,64,512]{2,1,0:T(8,128)(2,1)S(1)}, u32[]{:S(2)}, u32[]{:S(2)}) collective-permute-start(bf16[3,64,512]{2,1,0:T(8,128)(2,1)S(1)} %shard_map.69.mine), channel_id=1, source_target_pairs={{0,128},{16,144},{32,160},{48,176},{64,192},{80,208},{96,224},{112... | collective-permute-start | bytes 589832 | tf_op jit(solution)/shard_map/ppermute | solution.py:313
  260.9 3.8 %collective-permute-done.20.recv = bf16[3,64,512]{2,1,0:T(8,128)(2,1)S(1)} collective-permute-done((bf16[3,64,512]{2,1,0:T(8,128)(2,1)S(1)}, bf16[3,64,512]{2,1,0:T(8,128)(2,1)S(1)}, u32[]{:S(2)}, u32[]{:S(2)}) %collective-permute-start.20) | collective-permute-done | bytes 196640 | tf_op jit(solution)/shard_map/ppermute | solution.py:313
  265.7 1.9 collective-permute-start.21
  267.6 2.7 collective-permute-start.22
  270.3 3.5 %collective-permute-start.1 = (bf16[1,8,512]{2,1,0:T(8,128)(2,1)S(1)}, bf16[1,8,512]{2,1,0:T(8,128)(2,1)S(1)}, u32[]{:S(2)}, u32[]{:S(2)}) collective-permute-start(bf16[1,8,512]{2,1,0:T(8,128)(2,1)S(1)} %slice_bitcast_fusion.2), channel_id=1, source_target_pairs={{0,16},{16,32},{32,48},{48,64},{64,80},{80,96},{96,112},{112,128},... | collective-permute-start | bytes 24584 | tf_op jit(solution)/shard_map/ppermute | solution.py:313
  273.9 1.7 collective-permute-start.25
  275.6 2.7 collective-permute-done.22.refs_2_
  278.3 2.3 collective-permute-start.26
  281.3 1.9 shard_map.72.queries
  283.3 3.2 %shard_map.57.queries = bf16[1024,512]{1,0:T(8,128)(2,1)S(1)} custom-call(bf16[16,1,64,512]{3,2,1,0:T(8,128)(2,1)} %all-to-all-done.raw, bf16[1,8,512]{2,1,0:T(8,128)(2,1)S(1)} %collective-permute-done.tails, bf16[1,8,512]{2,1,0:T(8,128)(2,1)S(1)} %collective-permute-done.1.earlier.tails, f32[3,4,8192]{2,1,0:T(4,128)S(1)} %copy-done.8, ...), custom_call_target="tpu_custom_call" | custom-call | bytes 4194304 | tf_op jit(solution)/shard_map/pallas_call | solution.py:167
  286.5 3.5 %shard_map.73.rest_0_ = bf16[2,1024,512]{2,1,0:T(8,128)(2,1)} custom-call(bf16[1024,512]{1,0:T(8,128)(2,1)S(1)} %shard_map.72.queries, bf16[3,512,512]{2,1,0:T(8,128)(2,1)S(1)} %shard_map.66.weights), custom_call_target="tpu_custom_call" | custom-call | flops 1610612736 | bytes 4194304 | tf_op jit(solution)/shard_map/pallas_call | solution.py:300
  291.5 3.5 %shard_map.74 = bf16[2,1024,512]{2,1,0:T(8,128)(2,1)} custom-call(bf16[1024,512]{1,0:T(8,128)(2,1)S(1)} %shard_map.57.queries, bf16[3,512,512]{2,1,0:T(8,128)(2,1)S(1)} %shard_map.71.weights, bf16[2,1024,512]{2,1,0:T(8,128)(2,1)} %shard_map.73.rest_0_), custom_call_target="tpu_custom_call", output_to_operand_aliasing={{}: (2, {})} | custom-call | flops 1610612736 | bytes 4194304 | tf_op jit(solution)/shard_map/pallas_call | solution.py:300
  (80 shorter events, 19.7 us)
Async XLA Ops:
  0.0 2.8 copy-start
  4.2 37.7 %all-to-all-start.1 = ((bf16[16,1,64,512]{3,2,1,0:T(8,128)(2,1)}), bf16[16,1,64,512]{3,2,1,0:T(8,128)(2,1)S(1)}, u32[]{:S(2)}, u32[]{:S(2)}) async-start(bf16[16,1,64,512]{3,2,1,0:T(8,128)(2,1)} %shard_map.56), calls=%async_computation.1 | async-start | bytes 2097152 | tf_op jit(solution)/shard_map/all_to_all | solution.py:330
  15.8 2.8 copy-start.1
  22.3 1.4 copy-start.7
  41.9 47.1 %all-to-all-start.3 = ((bf16[16,2,64,512]{3,2,1,0:T(8,128)(2,1)}), bf16[16,2,64,512]{3,2,1,0:T(8,128)(2,1)S(1)}, u32[]{:S(2)}, u32[]{:S(2)}) async-start(bf16[16,2,64,512]{3,2,1,0:T(8,128)(2,1)} %copy-done.7), calls=%async_computation.3 | async-start | bytes 4194304 | tf_op jit(solution)/shard_map/all_to_all | solution.py:330
  48.5 2.8 copy-start.2
  55.0 1.3 copy-start.6
  56.4 54.4 %copy-start.8 = (f32[3,4,8192]{2,1,0:T(4,128)S(1)}, f32[3,4,8192]{2,1,0:T(4,128)}, u32[]{:S(2)}) copy-start(f32[3,4,8192]{2,1,0:T(4,128)} %taps.7) | copy-start | bytes 1179652
  89.0 1.4 copy-start.4
  90.4 114.4 %all-to-all-start.2 = ((bf16[16,2,64,512]{3,2,1,0:T(8,128)(2,1)}), bf16[16,2,64,512]{3,2,1,0:T(8,128)(2,1)S(1)}, u32[]{:S(2)}, u32[]{:S(2)}) async-start(bf16[16,2,64,512]{3,2,1,0:T(8,128)(2,1)} %copy-done.6), calls=%async_computation.2 | async-start | bytes 4194304 | tf_op jit(solution)/shard_map/all_to_all | solution.py:330
  105.2 5.6 %collective-permute-start.3 = (bf16[2,8,512]{2,1,0:T(8,128)(2,1)S(1)}, bf16[2,8,512]{2,1,0:T(8,128)(2,1)S(1)}, u32[]{:S(2)}, u32[]{:S(2)}) collective-permute-start(bf16[2,8,512]{2,1,0:T(8,128)(2,1)S(1)} %slice_bitcast_fusion), channel_id=1, source_target_pairs={{0,16},{16,32},{32,48},{48,64},{64,80},{80,96},{96,112},{112,128},... | collective-permute-start | bytes 49160 | tf_op jit(solution)/shard_map/ppermute | solution.py:313
  110.8 1.6 copy-start.5
  117.3 1.9 copy-start.15
  124.4 47.5 %collective-permute-start.4 = (bf16[4,3,64,512]{3,2,1,0:T(8,128)(2,1)S(1)}, bf16[4,3,64,512]{3,2,1,0:T(8,128)(2,1)S(1)}, u32[]{:S(2)}, u32[]{:S(2)}) collective-permute-start(bf16[4,3,64,512]{3,2,1,0:T(8,128)(2,1)S(1)} %get-tuple-element.30), channel_id=1, source_target_pairs={{0,16},{16,0},{32,48},{48,32},{64,80},{80,64},{96,112},{112,96},{1... | collective-permute-start | bytes 2359304 | tf_op jit(solution)/shard_map/ppermute | solution.py:313
  172.1 11.9 %collective-permute-start.5 = (bf16[3,64,512]{2,1,0:T(8,128)(2,1)S(1)}, bf16[3,64,512]{2,1,0:T(8,128)(2,1)S(1)}, u32[]{:S(2)}, u32[]{:S(2)}) collective-permute-start(bf16[3,64,512]{2,1,0:T(8,128)(2,1)S(1)} %get-tuple-element.32), channel_id=1, source_target_pairs={{0,32},{16,48},{32,64},{48,80},{64,96},{80,112},{96,0},{112,16},{1... | collective-permute-start | bytes 589832 | tf_op jit(solution)/shard_map/ppermute | solution.py:313
  172.2 11.8 %collective-permute-start.6 = (bf16[3,64,512]{2,1,0:T(8,128)(2,1)S(1)}, bf16[3,64,512]{2,1,0:T(8,128)(2,1)S(1)}, u32[]{:S(2)}, u32[]{:S(2)}) collective-permute-start(bf16[3,64,512]{2,1,0:T(8,128)(2,1)S(1)} %get-tuple-element.33), channel_id=1, source_target_pairs={{0,64},{16,80},{32,96},{48,112},{64,0},{80,16},{96,32},{112,48},{1... | collective-permute-start | bytes 589832 | tf_op jit(solution)/shard_map/ppermute | solution.py:313
  172.3 11.8 %collective-permute-start.7 = (bf16[3,64,512]{2,1,0:T(8,128)(2,1)S(1)}, bf16[3,64,512]{2,1,0:T(8,128)(2,1)S(1)}, u32[]{:S(2)}, u32[]{:S(2)}) collective-permute-start(bf16[3,64,512]{2,1,0:T(8,128)(2,1)S(1)} %get-tuple-element.34), channel_id=1, source_target_pairs={{0,96},{16,112},{32,0},{48,16},{64,32},{80,48},{96,64},{112,80},{1... | collective-permute-start | bytes 589832 | tf_op jit(solution)/shard_map/ppermute | solution.py:313
  184.8 5.3 %collective-permute-start.8 = (bf16[3,64,512]{2,1,0:T(8,128)(2,1)}, bf16[3,64,512]{2,1,0:T(8,128)(2,1)}, u32[]{:S(2)}, u32[]{:S(2)}) collective-permute-start(bf16[3,64,512]{2,1,0:T(8,128)(2,1)} %shard_map.64.mine), channel_id=1, source_target_pairs={{0,128},{16,144},{32,160},{48,176},{64,192},{80,208},{96,224},{112... | collective-permute-start | bytes 589832 | tf_op jit(solution)/shard_map/ppermute | solution.py:313
  190.1 1.0 copy-start.10
  193.0 0.8 copy-start.11
  194.5 20.2 %collective-permute-start.9 = (bf16[3,64,512]{2,1,0:T(8,128)(2,1)}, bf16[3,64,512]{2,1,0:T(8,128)(2,1)}, u32[]{:S(2)}, u32[]{:S(2)}) collective-permute-start(bf16[3,64,512]{2,1,0:T(8,128)(2,1)} %get-tuple-element.35.refs_0_), channel_id=1, source_target_pairs={{0,32},{16,48},{32,64},{48,80},{64,96},{80,112},{96,0},{112,16},{1... | collective-permute-start | bytes 589832 | tf_op jit(solution)/shard_map/ppermute | solution.py:313
  196.4 18.4 %collective-permute-start.10 = (bf16[3,64,512]{2,1,0:T(8,128)(2,1)}, bf16[3,64,512]{2,1,0:T(8,128)(2,1)}, u32[]{:S(2)}, u32[]{:S(2)}) collective-permute-start(bf16[3,64,512]{2,1,0:T(8,128)(2,1)} %get-tuple-element.35.refs_0_), channel_id=1, source_target_pairs={{0,64},{16,80},{32,96},{48,112},{64,0},{80,16},{96,32},{112,48},{1... | collective-permute-start | bytes 589832 | tf_op jit(solution)/shard_map/ppermute | solution.py:313
  199.1 16.1 %collective-permute-start.11 = (bf16[3,64,512]{2,1,0:T(8,128)(2,1)}, bf16[3,64,512]{2,1,0:T(8,128)(2,1)}, u32[]{:S(2)}, u32[]{:S(2)}) collective-permute-start(bf16[3,64,512]{2,1,0:T(8,128)(2,1)} %get-tuple-element.35.refs_0_), channel_id=1, source_target_pairs={{0,96},{16,112},{32,0},{48,16},{64,32},{80,48},{96,64},{112,80},{1... | collective-permute-start | bytes 589832 | tf_op jit(solution)/shard_map/ppermute | solution.py:313
  199.1 2.8 copy-start.3
  203.8 1.0 copy-start.9
  204.7 75.8 %all-to-all-start = ((bf16[16,1,64,512]{3,2,1,0:T(8,128)(2,1)}), bf16[16,1,64,512]{3,2,1,0:T(8,128)(2,1)}, u32[]{:S(2)}, u32[]{:S(2)}) async-start(bf16[16,1,64,512]{3,2,1,0:T(8,128)(2,1)} %copy-done.9), calls=%async_computation | async-start | bytes 2097152 | tf_op jit(solution)/shard_map/all_to_all | solution.py:330
  212.2 11.1 %collective-permute-start.12 = (bf16[3,64,512]{2,1,0:T(8,128)(2,1)}, bf16[3,64,512]{2,1,0:T(8,128)(2,1)S(1)}, u32[]{:S(2)}, u32[]{:S(2)}) collective-permute-start(bf16[3,64,512]{2,1,0:T(8,128)(2,1)} %get-tuple-element.35.refs_0_), channel_id=1, source_target_pairs={{0,16},{16,0},{32,48},{48,32},{64,80},{80,64},{96,112},{112,96},{1... | collective-permute-start | bytes 589832 | tf_op jit(solution)/shard_map/ppermute | solution.py:313
  214.7 8.5 %collective-permute-start.13 = (bf16[3,64,512]{2,1,0:T(8,128)(2,1)}, bf16[3,64,512]{2,1,0:T(8,128)(2,1)S(1)}, u32[]{:S(2)}, u32[]{:S(2)}) collective-permute-start(bf16[3,64,512]{2,1,0:T(8,128)(2,1)} %collective-permute-done.9.refs_1_), channel_id=1, source_target_pairs={{0,16},{16,0},{32,48},{48,32},{64,80},{80,64},{96,112},{112,96},{1... | collective-permute-start | bytes 589832 | tf_op jit(solution)/shard_map/ppermute | solution.py:313
  214.8 8.4 %collective-permute-start.14 = (bf16[3,64,512]{2,1,0:T(8,128)(2,1)}, bf16[3,64,512]{2,1,0:T(8,128)(2,1)S(1)}, u32[]{:S(2)}, u32[]{:S(2)}) collective-permute-start(bf16[3,64,512]{2,1,0:T(8,128)(2,1)} %collective-permute-done.10.refs_2_), channel_id=1, source_target_pairs={{0,16},{16,0},{32,48},{48,32},{64,80},{80,64},{96,112},{112,96},{1... | collective-permute-start | bytes 589832 | tf_op jit(solution)/shard_map/ppermute | solution.py:313
  215.2 8.0 %collective-permute-start.15 = (bf16[3,64,512]{2,1,0:T(8,128)(2,1)}, bf16[3,64,512]{2,1,0:T(8,128)(2,1)S(1)}, u32[]{:S(2)}, u32[]{:S(2)}) collective-permute-start(bf16[3,64,512]{2,1,0:T(8,128)(2,1)} %collective-permute-done.11.refs_3_), channel_id=1, source_target_pairs={{0,16},{16,0},{32,48},{48,32},{64,80},{80,64},{96,112},{112,96},{1... | collective-permute-start | bytes 589832 | tf_op jit(solution)/shard_map/ppermute | solution.py:313
  215.4 2.9 collective-permute-start.2
  230.2 34.5 %copy-start.12 = (f32[3,64,512]{2,1,0:T(8,128)S(1)}, f32[3,64,512]{2,1,0:T(8,128)}, u32[]{:S(2)}) copy-start(f32[3,64,512]{2,1,0:T(8,128)} %copy-done.11) | copy-start | bytes 1179652
  230.2 34.5 %copy-start.14 = (f32[3,64,512]{2,1,0:T(8,128)S(1)}, f32[3,64,512]{2,1,0:T(8,128)}, u32[]{:S(2)}) copy-start(f32[3,64,512]{2,1,0:T(8,128)} %copy-done.13) | copy-start | bytes 1179652
  230.2 51.1 %copy-start.18 = (f32[2,1,512]{2,1,0:T(1,128)S(1)}, f32[2,1,512]{2,1,0:T(1,128)}, u32[]{:S(2)}) copy-start(f32[2,1,512]{2,1,0:T(1,128)} %gain.7) | copy-start | bytes 12292
  230.2 13.0 %collective-permute-start.16 = (bf16[4,3,64,512]{3,2,1,0:T(8,128)(2,1)S(1)}, bf16[4,3,64,512]{3,2,1,0:T(8,128)(2,1)S(1)}, u32[]{:S(2)}, u32[]{:S(2)}) collective-permute-start(bf16[4,3,64,512]{3,2,1,0:T(8,128)(2,1)S(1)} %get-tuple-element.37), channel_id=1, source_target_pairs={{0,16},{16,0},{32,48},{48,32},{64,80},{80,64},{96,112},{112,96},{1... | collective-permute-start | bytes 2359304 | tf_op jit(solution)/shard_map/ppermute | solution.py:313
  243.4 8.6 %collective-permute-start.17 = (bf16[3,64,512]{2,1,0:T(8,128)(2,1)S(1)}, bf16[3,64,512]{2,1,0:T(8,128)(2,1)S(1)}, u32[]{:S(2)}, u32[]{:S(2)}) collective-permute-start(bf16[3,64,512]{2,1,0:T(8,128)(2,1)S(1)} %get-tuple-element.39), channel_id=1, source_target_pairs={{0,32},{16,48},{32,64},{48,80},{64,96},{80,112},{96,0},{112,16},{1... | collective-permute-start | bytes 589832 | tf_op jit(solution)/shard_map/ppermute | solution.py:313
  243.5 13.6 %collective-permute-start.18 = (bf16[3,64,512]{2,1,0:T(8,128)(2,1)S(1)}, bf16[3,64,512]{2,1,0:T(8,128)(2,1)S(1)}, u32[]{:S(2)}, u32[]{:S(2)}) collective-permute-start(bf16[3,64,512]{2,1,0:T(8,128)(2,1)S(1)} %get-tuple-element.40), channel_id=1, source_target_pairs={{0,64},{16,80},{32,96},{48,112},{64,0},{80,16},{96,32},{112,48},{1... | collective-permute-start | bytes 589832 | tf_op jit(solution)/shard_map/ppermute | solution.py:313
  248.1 9.1 %collective-permute-start.19 = (bf16[3,64,512]{2,1,0:T(8,128)(2,1)S(1)}, bf16[3,64,512]{2,1,0:T(8,128)(2,1)S(1)}, u32[]{:S(2)}, u32[]{:S(2)}) collective-permute-start(bf16[3,64,512]{2,1,0:T(8,128)(2,1)S(1)} %get-tuple-element.41), channel_id=1, source_target_pairs={{0,96},{16,112},{32,0},{48,16},{64,32},{80,48},{96,64},{112,80},{1... | collective-permute-start | bytes 589832 | tf_op jit(solution)/shard_map/ppermute | solution.py:313
  257.2 7.5 %collective-permute-start.20 = (bf16[3,64,512]{2,1,0:T(8,128)(2,1)S(1)}, bf16[3,64,512]{2,1,0:T(8,128)(2,1)S(1)}, u32[]{:S(2)}, u32[]{:S(2)}) collective-permute-start(bf16[3,64,512]{2,1,0:T(8,128)(2,1)S(1)} %shard_map.69.mine), channel_id=1, source_target_pairs={{0,128},{16,144},{32,160},{48,176},{64,192},{80,208},{96,224},{112... | collective-permute-start | bytes 589832 | tf_op jit(solution)/shard_map/ppermute | solution.py:313
  265.7 8.2 %collective-permute-start.21 = (bf16[3,64,512]{2,1,0:T(8,128)(2,1)S(1)}, bf16[3,64,512]{2,1,0:T(8,128)(2,1)S(1)}, u32[]{:S(2)}, u32[]{:S(2)}) collective-permute-start(bf16[3,64,512]{2,1,0:T(8,128)(2,1)S(1)} %get-tuple-element.44.refs_0_), channel_id=1, source_target_pairs={{0,32},{16,48},{32,64},{48,80},{64,96},{80,112},{96,0},{112,16},{1... | collective-permute-start | bytes 589832 | tf_op jit(solution)/shard_map/ppermute | solution.py:313
  267.6 10.7 %collective-permute-start.22 = (bf16[3,64,512]{2,1,0:T(8,128)(2,1)S(1)}, bf16[3,64,512]{2,1,0:T(8,128)(2,1)}, u32[]{:S(2)}, u32[]{:S(2)}) collective-permute-start(bf16[3,64,512]{2,1,0:T(8,128)(2,1)S(1)} %get-tuple-element.44.refs_0_), channel_id=1, source_target_pairs={{0,64},{16,80},{32,96},{48,112},{64,0},{80,16},{96,32},{112,48},{1... | collective-permute-start | bytes 589832 | tf_op jit(solution)/shard_map/ppermute | solution.py:313
  270.3 10.3 %collective-permute-start.23 = (bf16[3,64,512]{2,1,0:T(8,128)(2,1)S(1)}, bf16[3,64,512]{2,1,0:T(8,128)(2,1)}, u32[]{:S(2)}, u32[]{:S(2)}) collective-permute-start(bf16[3,64,512]{2,1,0:T(8,128)(2,1)S(1)} %get-tuple-element.44.refs_0_), channel_id=1, source_target_pairs={{0,96},{16,112},{32,0},{48,16},{64,32},{80,48},{96,64},{112,80},{1... | collective-permute-start | bytes 589832 | tf_op jit(solution)/shard_map/ppermute | solution.py:313
  270.3 11.0 %collective-permute-start.1 = (bf16[1,8,512]{2,1,0:T(8,128)(2,1)S(1)}, bf16[1,8,512]{2,1,0:T(8,128)(2,1)S(1)}, u32[]{:S(2)}, u32[]{:S(2)}) collective-permute-start(bf16[1,8,512]{2,1,0:T(8,128)(2,1)S(1)} %slice_bitcast_fusion.2), channel_id=1, source_target_pairs={{0,16},{16,32},{32,48},{48,64},{64,80},{80,96},{96,112},{112,128},... | collective-permute-start | bytes 24584 | tf_op jit(solution)/shard_map/ppermute | solution.py:313
  273.9 16.1 %collective-permute-start.24 = (bf16[3,64,512]{2,1,0:T(8,128)(2,1)S(1)}, bf16[3,64,512]{2,1,0:T(8,128)(2,1)}, u32[]{:S(2)}, u32[]{:S(2)}) collective-permute-start(bf16[3,64,512]{2,1,0:T(8,128)(2,1)S(1)} %get-tuple-element.44.refs_0_), channel_id=1, source_target_pairs={{0,16},{16,0},{32,48},{48,32},{64,80},{80,64},{96,112},{112,96},{1... | collective-permute-start | bytes 589832 | tf_op jit(solution)/shard_map/ppermute | solution.py:313
  273.9 16.1 %collective-permute-start.25 = (bf16[3,64,512]{2,1,0:T(8,128)(2,1)S(1)}, bf16[3,64,512]{2,1,0:T(8,128)(2,1)}, u32[]{:S(2)}, u32[]{:S(2)}) collective-permute-start(bf16[3,64,512]{2,1,0:T(8,128)(2,1)S(1)} %collective-permute-done.21.refs_1_), channel_id=1, source_target_pairs={{0,16},{16,0},{32,48},{48,32},{64,80},{80,64},{96,112},{112,96},{1... | collective-permute-start | bytes 589832 | tf_op jit(solution)/shard_map/ppermute | solution.py:313
  278.3 11.7 %collective-permute-start.26 = (bf16[3,64,512]{2,1,0:T(8,128)(2,1)}, bf16[3,64,512]{2,1,0:T(8,128)(2,1)}, u32[]{:S(2)}, u32[]{:S(2)}) collective-permute-start(bf16[3,64,512]{2,1,0:T(8,128)(2,1)} %collective-permute-done.22.refs_2_), channel_id=1, source_target_pairs={{0,16},{16,0},{32,48},{48,32},{64,80},{80,64},{96,112},{112,96},{1... | collective-permute-start | bytes 589832 | tf_op jit(solution)/shard_map/ppermute | solution.py:313
  280.6 9.4 %collective-permute-start.27 = (bf16[3,64,512]{2,1,0:T(8,128)(2,1)}, bf16[3,64,512]{2,1,0:T(8,128)(2,1)}, u32[]{:S(2)}, u32[]{:S(2)}) collective-permute-start(bf16[3,64,512]{2,1,0:T(8,128)(2,1)} %collective-permute-done.23.refs_3_), channel_id=1, source_target_pairs={{0,16},{16,0},{32,48},{48,32},{64,80},{80,64},{96,112},{112,96},{1... | collective-permute-start | bytes 589832 | tf_op jit(solution)/shard_map/ppermute | solution.py:313
  281.3 2.0 collective-permute-start
  (3 other events, 2.1 us)

commit v2 on v1

--- a/solution.py
+++ b/solution.py
@@ -88,9 +88,20 @@
 
 
 def conv_chunk(raw, stream, n, edge, taps):
-    current = raw[pl.ds(LEAD * n, LEAD), stream].reshape(CHUNK, HEAD).astype(F32)
-    inner = raw[jnp.maximum(LEAD * n - 1, 0), stream, 48:64, :].astype(F32)[8:]
+    current = raw[stream, pl.ds(LEAD * n, LEAD)].reshape(CHUNK, HEAD).astype(F32)
+    inner = raw[stream, jnp.maximum(LEAD * n - 1, 0), 48:64, :].astype(F32)[8:]
     return conv_silu(current, jnp.where(n == 0, edge, inner), taps)
+
+
+def raw_copy(source, raw, sems, offset, stream, n):
+    lead = pl.ds(LEAD * n, LEAD)
+    return pltpu.make_async_copy(
+        source.at[lead, offset + stream], raw.at[stream, lead], sems.at[stream, n]
+    )
+
+
+def raw_scratch(streams):
+    return [pltpu.VMEM((streams, 16, 64, HEAD), BF), pltpu.SemaphoreType.DMA((streams, BLOCKS))]
 
 
 def chunk_rows(n):
@@ -101,72 +112,107 @@
     return pl.BlockSpec(memory_space=pltpu.HBM)
 
 
-def spread_of(first_stream, streams, group):
+def in_hbm(value):
+    return pltpu.with_memory_space_constraint(value, pltpu.HBM)
+
+
+def spread(source, spots):
     def body(source, out, stage, sems_in, sems_out):
         def pull(s, h):
+            stream, group = spots[s]
             cols = pl.ds(h * HEAD, HEAD)
-            spot = source.at[first_stream + s, group, :, cols]
-            return pltpu.make_async_copy(spot, stage.at[s, h], sems_in.at[s, h])
+            return pltpu.make_async_copy(
+                source.at[stream, group, :, cols], stage.at[h, s], sems_in.at[s, h]
+            )
 
         def push(s, h):
-            return pltpu.make_async_copy(stage.at[s, h], out.at[h, s], sems_out.at[s, h])
-
-        spots = [(s, h) for s in range(streams) for h in range(16)]
-        for spot in spots:
+            return pltpu.make_async_copy(stage.at[h, s], out.at[h, s], sems_out.at[s, h])
+
+        both = [(s, h) for s in range(2) for h in range(16)]
+        for spot in both:
             pull(*spot).start()
-        for spot in spots:
+        for spot in both:
             pull(*spot).wait()
             push(*spot).start()
-        for spot in spots:
+        for spot in both:
             push(*spot).wait()
 
     return call(
         body,
-        sds((16, streams, 64, HEAD), BF),
+        sds((16, 2, 64, HEAD), BF),
         [hbm()],
         [
-            pltpu.VMEM((streams, 16, 64, HEAD), BF),
-            pltpu.SemaphoreType.DMA((streams, 16)),
-            pltpu.SemaphoreType.DMA((streams, 16)),
+            pltpu.VMEM((16, 2, 64, HEAD), BF),
+            pltpu.SemaphoreType.DMA((2, 16)),
+            pltpu.SemaphoreType.DMA((2, 16)),
         ],
-        nbytes=streams << 21,
+        nbytes=4 << 20,
         out_specs=hbm(),
-    )
-
-
-def prepare(first, raw, tails, earlier, taps, gain):
-    def body(raw, tails, earlier, taps, gain, keys, values):
+        limit=60,
+    )(in_hbm(source))
+
+
+def prepare(first, source, tails, earlier, taps, gain, start):
+    def body(source, tails, earlier, taps, gain, *rest):
+        if first:
+            start, keys, values, narrow, raw, sems, wide, wide_sem = rest
+        else:
+            keys, values, raw, sems = rest
+        for n in range(BLOCKS):
+            for stream in range(2):
+                raw_copy(source, raw, sems, 0, stream, n).start()
+        if first:
+            fetch = pltpu.make_async_copy(start, wide, wide_sem)
+            fetch.start()
         key_taps, value_taps = own_taps(taps, 1), own_taps(taps, 2)
         key_edge = edge_rows(first, tails, earlier, 0)
         value_edge = edge_rows(first, tails, earlier, 1)
 
         def step(n, carry):
             rows = chunk_rows(n)
+            raw_copy(source, raw, sems, 0, 0, n).wait()
+            raw_copy(source, raw, sems, 0, 1, n).wait()
             keys[rows, :] = rms_scaled(conv_chunk(raw, 0, n, key_edge, key_taps), gain[1])
             act = conv_chunk(raw, 1, n, value_edge, value_taps)
             values[rows, :] = (act.astype(F32) * (-1.0 / 16384)).astype(BF)
             return carry
 
         lax.fori_loop(0, BLOCKS, step, 0)
+        if first:
+            fetch.wait()
+            narrow[...] = wide[...].astype(BF)
 
     rows = sds((ROWS, HEAD), BF)
-    return call(body, [rows, rows], [vmem()] * 5, nbytes=8 << 20)(raw, tails, earlier, taps, gain)
-
-
-def prepare_queries(first, raw, tails, earlier, taps, gain):
-    def body(raw, tails, earlier, taps, gain, queries):
+    square = (3, HEAD, HEAD)
+    outs = [rows, rows] + ([sds(square, BF)] if first else [])
+    scratch = raw_scratch(2) + ([pltpu.VMEM(square, F32), pltpu.SemaphoreType.DMA(())] if first else [])
+    ins = [in_hbm(source), tails, earlier, taps, gain] + ([in_hbm(start)] if first else [])
+    specs = [hbm()] + [vmem()] * 4 + ([hbm()] if first else [])
+    return call(body, outs, specs, scratch, nbytes=8 << 20, limit=24)(*ins)
+
+
+def prepare_queries(source, tails, taps, gain):
+    def body(source, tails, taps, gain, *rest):
+        raw, sems = rest[-2:]
+        for group in range(GROUPS):
+            for n in range(BLOCKS):
+                raw_copy(source, raw, sems, 0, group, n).start()
         query_taps = own_taps(taps, 0)
-        edge = edge_rows(first, tails, earlier, 0)
-
-        def step(n, carry):
-            queries[chunk_rows(n), :] = rms_scaled(conv_chunk(raw, 0, n, edge, query_taps), gain[0])
-            return carry
-
-        lax.fori_loop(0, BLOCKS, step, 0)
-
-    return call(body, sds((ROWS, HEAD), BF), [vmem()] * 5, nbytes=4 << 20)(
-        raw, tails, earlier, taps, gain
-    )
+        for group, queries in enumerate(rest[:GROUPS]):
+            edge = edge_rows(group == 0, tails.at[group : group + 1], tails, 0)
+
+            def step(n, carry, group=group, queries=queries, edge=edge):
+                raw_copy(source, raw, sems, 0, group, n).wait()
+                act = conv_chunk(raw, group, n, edge, query_taps)
+                queries[chunk_rows(n), :] = rms_scaled(act, gain[0])
+                return carry
+
+            lax.fori_loop(0, BLOCKS, step, 0)
+
+    rows = sds((ROWS, HEAD), BF)
+    return call(
+        body, [rows, rows], [hbm()] + [vmem()] * 3, raw_scratch(GROUPS), nbytes=8 << 20
+    )(in_hbm(source), tails, taps, gain)
 
 
 def gradients(keys, values, weights, plain):
@@ -325,9 +371,9 @@
     return seq_permute(value, lambda i: (i & 9) | (((i >> 1 & 3) + d & 3) << 1))
 
 
-def regroup(qkv_proj, first_stream, streams, group):
-    spread = spread_of(first_stream, streams, group)(qkv_proj)
-    return lax.all_to_all(spread, "wide", 0, 0, tiled=True)
+def regroup(qkv_proj, spots):
+    ready = spread(qkv_proj, spots)
+    return lax.all_to_all(ready, "wide", 0, 0, tiled=True)
 
 
 def tails_behind(raw):
@@ -356,26 +402,23 @@
     own_at = (seq & 1) * 256 + (seq >> 1 & 3) * 64
     state = jnp.swapaxes(lax.dynamic_slice_in_dim(start, own_at, 64, 2), 1, 2)
 
-    kv0 = regroup(qkv_proj, 1, 2, 0)
+    kv0 = regroup(qkv_proj, ((1, 0), (2, 0)))
     tails0 = tails_behind(kv0)
-    kv1 = regroup(qkv_proj, 1, 2, 1)
+    kv1 = regroup(qkv_proj, ((1, 1), (2, 1)))
     tails1 = tails_behind(kv1)
-    q0 = regroup(qkv_proj, 0, 1, 0)
-    qtails0 = tails_behind(q0)
-    q1 = regroup(qkv_proj, 0, 1, 1)
-    qtails1 = tails_behind(q1)
-
-    keys, values = prepare(True, kv0, tails0, tails0, conv_kernel, qk_gain)
-    mine, recv = reduce_pieces(*gradients(keys, values, start, True))
+    q = regroup(qkv_proj, ((0, 0), (0, 1)))
+    qtails = tails_behind(q)
+
+    keys, values, narrow = prepare(True, kv0, tails0, tails0, conv_kernel, qk_gain, start)
+    mine, recv = reduce_pieces(*gradients(keys, values, narrow, True))
     moment, state, narrow = update(step_size, mine, recv, state, None)
     weights1 = assemble(gather_pieces(narrow))
-    keys, values = prepare(False, kv1, tails1, tails0, conv_kernel, qk_gain)
+    keys, values = prepare(False, kv1, tails1, tails0, conv_kernel, qk_gain, None)
     mine, recv = reduce_pieces(*gradients(keys, values, weights1, False))
     moment, state, narrow = update(step_size, mine, recv, state, moment)
     weights2 = assemble(gather_pieces(narrow))
-    queries0 = prepare_queries(True, q0, qtails0, qtails0, conv_kernel, qk_gain)
+    queries0, queries1 = prepare_queries(q, qtails, conv_kernel, qk_gain)
     out = apply_fast(queries0, weights1, 0, None)
-    queries1 = prepare_queries(False, q1, qtails1, qtails0, conv_kernel, qk_gain)
     return apply_fast(queries1, weights2, 1, out)
 
 

time: 300 us -> 295 us (0.983)
  waiting for transfers between devices: 81.4 us -> 121 us
  local copies, waits for them, and re-layouts: 29.4 us -> 6.53 us
  starting transfers between devices: 134 us -> 116 us
  Pallas kernels: 49 us -> 44.2 us
    all_to_all x4 -> x3, waiting for transfers between devices: 50.9 us -> 84.8 us  [regroup(): return lax.all_to_all(ready, 'wide', 0, 0, tiled=True)]
    unnamed x38 -> x8, local copies, waits for them, and re-layouts: 23.5 us -> 2.72 us
    ppermute x28 -> x27, starting transfers between devices: 94.5 us -> 84.9 us  [seq_permute(): return lax.ppermute(value, 'seq', [(i, target(i)) for i in range(16)])]
    all_to_all x4 -> x3, starting transfers between devices: 39.7 us -> 31 us  [regroup(): return lax.all_to_all(ready, 'wide', 0, 0, tiled=True)]
    ppermute x28 -> x27, waiting for transfers between devices: 30.5 us -> 36.5 us  [seq_permute(): return lax.ppermute(value, 'seq', [(i, target(i)) for i in range(16)])]
    pallas_call x8 -> x6, Pallas kernels: 24.4 us -> 24.2 us  [the longest x2 11 us: prepare(): return call(body, outs, specs, scratch, nbytes=8 << 20, limit=24)(*ins)]
  transfers between devices with their start and end apart: 32 -> 30, of which waited for: 12 -> 14; matrix products, arithmetic and copies ran while one was open for 2% -> 1% of each run, Pallas kernels for 14% -> 13%
where the time goes in v2:
time: 295 us; the launch traced here: 289 us
  waiting for transfers between devices  121 us (41%)
  starting transfers between devices  116 us (39%)
  Pallas kernels  44.2 us (15%)
  local copies, waits for them, and re-layouts  6.53 us (2%)
    ppermute x27, starting transfers between devices, seq_permute(): return lax.ppermute(value, 'seq', [(i, target(i)) for i in range(16)])  84.9 us
    all_to_all x3, waiting for transfers between devices, regroup(): return lax.all_to_all(ready, 'wide', 0, 0, tiled=True)  84.8 us
    ppermute x27, waiting for transfers between devices, seq_permute(): return lax.ppermute(value, 'seq', [(i, target(i)) for i in range(16)])  36.5 us
    all_to_all x3, starting transfers between devices, regroup(): return lax.all_to_all(ready, 'wide', 0, 0, tiled=True)  31 us
    pallas_call x2, Pallas kernels, gradients(): call(body, [half, half], [vmem()] * 3, [pltpu.VMEM((ROWS, HEAD), BF)] * 3...  11.1 us
    pallas_call x2, Pallas kernels, prepare(): return call(body, outs, specs, scratch, nbytes=8 << 20, limit=24)(*ins)  11 us
    pallas_call x3, Pallas kernels, spread(): call(body, sds((16, 2, 64, HEAD), BF), [hbm()], [pltpu.VMEM((16, 2, 64, H...  8.37 us
    pallas_call x2, Pallas kernels, apply_fast(): call(body, sds((GROUPS, ROWS, HEAD), BF), [vmem()] * 2 + [anywhere()] * l...  7.01 us
  transfers between devices with their start and end apart: 30, of which 14 were waited for; matrix products, arithmetic and copies ran while one was open for 1% of the time, Pallas kernels for 13%

profile of v2, /device:TPU:1, one launch (start us, length us, event | category | flops | bytes accessed | tf_op | source)
XLA Modules:
  0.0 289.1 jit_solution(3499004820051979376)
XLA Ops:
  0.0 2.8 shard_map.58
  2.8 11.6 %all-to-all-start.2 = ((bf16[16,2,64,512]{3,2,1,0:T(8,128)(2,1)}), bf16[16,2,64,512]{3,2,1,0:T(8,128)(2,1)S(1)}, u32[]{:S(2)}, u32[]{:S(2)}) async-start(bf16[16,2,64,512]{3,2,1,0:T(8,128)(2,1)} %shard_map.58), calls=%async_computation.2 | async-start | bytes 4194304 | tf_op jit(solution)/shard_map/all_to_all | solution.py:376
  14.4 2.8 shard_map.57
  17.2 44.6 %all-to-all-done.2.source = bf16[16,2,64,512]{3,2,1,0:T(8,128)(2,1)S(1)} async-done(((bf16[16,2,64,512]{3,2,1,0:T(8,128)(2,1)}), bf16[16,2,64,512]{3,2,1,0:T(8,128)(2,1)S(1)}, u32[]{:S(2)}, u32[]{:S(2)}) %all-to-all-start.2) | async-done | bytes 2097184 | tf_op jit(solution)/shard_map/all_to_all | solution.py:376
  61.8 1.3 copy-done.3
  63.1 7.8 %all-to-all-start.1 = ((bf16[16,2,64,512]{3,2,1,0:T(8,128)(2,1)}), bf16[16,2,64,512]{3,2,1,0:T(8,128)(2,1)S(1)}, u32[]{:S(2)}, u32[]{:S(2)}) async-start(bf16[16,2,64,512]{3,2,1,0:T(8,128)(2,1)} %shard_map.57), calls=%async_computation.1 | async-start | bytes 4194304 | tf_op jit(solution)/shard_map/all_to_all | solution.py:376
  70.9 2.8 shard_map.55
  73.7 40.2 %all-to-all-done.1.source = bf16[16,2,64,512]{3,2,1,0:T(8,128)(2,1)S(1)} async-done(((bf16[16,2,64,512]{3,2,1,0:T(8,128)(2,1)}), bf16[16,2,64,512]{3,2,1,0:T(8,128)(2,1)S(1)}, u32[]{:S(2)}, u32[]{:S(2)}) %all-to-all-start.1) | async-done | bytes 2097184 | tf_op jit(solution)/shard_map/all_to_all | solution.py:376
  113.9 1.4 copy-done.2
  115.3 11.7 %all-to-all-start = ((bf16[16,2,64,512]{3,2,1,0:T(8,128)(2,1)}), bf16[16,2,64,512]{3,2,1,0:T(8,128)(2,1)}, u32[]{:S(2)}, u32[]{:S(2)}) async-start(bf16[16,2,64,512]{3,2,1,0:T(8,128)(2,1)} %shard_map.55), calls=%async_computation | async-start | bytes 4194304 | tf_op jit(solution)/shard_map/all_to_all | solution.py:376
  127.0 0.7 slice_bitcast_fusion
  127.7 5.5 %collective-permute-start.2 = (bf16[2,8,512]{2,1,0:T(8,128)(2,1)S(1)}, bf16[2,8,512]{2,1,0:T(8,128)(2,1)S(1)}, u32[]{:S(2)}, u32[]{:S(2)}) collective-permute-start(bf16[2,8,512]{2,1,0:T(8,128)(2,1)S(1)} %slice_bitcast_fusion), channel_id=1, source_target_pairs={{0,16},{16,32},{32,48},{48,64},{64,80},{80,96},{96,112},{112,128},... | collective-permute-start | bytes 49160 | tf_op jit(solution)/shard_map/ppermute | solution.py:359
  133.2 0.9 collective-permute-done.2.earlier.tails
  134.0 5.6 %shard_map.60 = (bf16[1024,512]{1,0:T(8,128)(2,1)S(1)}, bf16[1024,512]{1,0:T(8,128)(2,1)S(1)}, bf16[3,512,512]{2,1,0:T(8,128)(2,1)S(1)}) custom-call(bf16[16,2,64,512]{3,2,1,0:T(8,128)(2,1)} %copy-done.3, bf16[2,8,512]{2,1,0:T(8,128)(2,1)S(1)} %collective-permute-done.2.earlier.tails, bf16[2,8,512]{2,1,0:T(8,128)(2,1)S(1)} %collective-permute-done.2.earlier.tails, ...), custom_call_target="tpu_custom_call" | custom-call | bytes 8388608 | tf_op jit(solution)/shard_map/pallas_call | solution.py:191
  139.6 5.5 %shard_map.61 = (bf16[4,3,64,512]{3,2,1,0:T(8,128)(2,1)S(1)}, bf16[4,3,64,512]{3,2,1,0:T(8,128)(2,1)S(1)}) custom-call(bf16[1024,512]{1,0:T(8,128)(2,1)S(1)} %get-tuple-element.31.keys, bf16[1024,512]{1,0:T(8,128)(2,1)S(1)} %get-tuple-element.32.values, bf16[3,512,512]{2,1,0:T(8,128)(2,1)S(1)} %get-tuple-element.33.weights), custom_call_target="tpu_custom_call" | custom-call | flops 3221225472 | bytes 4194304 | tf_op jit(solution)/shard_map/pallas_call | solution.py:253
  145.1 43.0 %collective-permute-start.3 = (bf16[4,3,64,512]{3,2,1,0:T(8,128)(2,1)S(1)}, bf16[4,3,64,512]{3,2,1,0:T(8,128)(2,1)S(1)}, u32[]{:S(2)}, u32[]{:S(2)}) collective-permute-start(bf16[4,3,64,512]{3,2,1,0:T(8,128)(2,1)S(1)} %get-tuple-element.35), channel_id=1, source_target_pairs={{0,16},{16,0},{32,48},{48,32},{64,80},{80,64},{96,112},{112,96},{1... | collective-permute-start | bytes 2359304 | tf_op jit(solution)/shard_map/ppermute | solution.py:359
  188.1 1.9 collective-permute-done.3.recv
  190.4 2.6 collective-permute-start.6
  193.0 9.2 %collective-permute-done.4.one = bf16[3,64,512]{2,1,0:T(8,128)(2,1)S(1)} collective-permute-done((bf16[3,64,512]{2,1,0:T(8,128)(2,1)S(1)}, bf16[3,64,512]{2,1,0:T(8,128)(2,1)S(1)}, u32[]{:S(2)}, u32[]{:S(2)}) %collective-permute-start.4) | collective-permute-done | bytes 196640 | tf_op jit(solution)/shard_map/ppermute | solution.py:359
  202.4 1.4 constant_dynamic-slice_fusion
  204.7 2.7 collective-permute-done.7.recv
  207.5 2.0 collective-permute-start.8
  209.5 2.7 collective-permute-start.9
  212.2 2.2 collective-permute-start.11
  214.5 3.3 %collective-permute-start.12 = (bf16[3,64,512]{2,1,0:T(8,128)(2,1)S(1)}, bf16[3,64,512]{2,1,0:T(8,128)(2,1)S(1)}, u32[]{:S(2)}, u32[]{:S(2)}) collective-permute-start(bf16[3,64,512]{2,1,0:T(8,128)(2,1)S(1)} %collective-permute-done.8.refs_1_), channel_id=1, source_target_pairs={{0,16},{16,0},{32,48},{48,32},{64,80},{80,64},{96,112},{112,96},{1... | collective-permute-start | bytes 589832 | tf_op jit(solution)/shard_map/ppermute | solution.py:359
  217.8 2.0 collective-permute-done.9.refs_2_
  219.8 2.5 collective-permute-start.13
  222.3 0.7 slice_bitcast_fusion.1
  223.3 0.9 collective-permute-done.1.tails
  224.2 5.4 %shard_map.59 = (bf16[1024,512]{1,0:T(8,128)(2,1)S(1)}, bf16[1024,512]{1,0:T(8,128)(2,1)S(1)}) custom-call(bf16[16,2,64,512]{3,2,1,0:T(8,128)(2,1)} %copy-done.2, bf16[2,8,512]{2,1,0:T(8,128)(2,1)S(1)} %collective-permute-done.1.tails, bf16[2,8,512]{2,1,0:T(8,128)(2,1)S(1)} %collective-permute-done.2.earlier.tails, f32[3,4,8192]{2,1,0:T(4,128)S(1)} %copy-done, ...), custom_call_target="tpu_custom_call" | custom-call | bytes 8388608 | tf_op jit(solution)/shard_map/pallas_call | solution.py:191
  229.8 5.6 %shard_map.66 = (bf16[4,3,64,512]{3,2,1,0:T(8,128)(2,1)S(1)}, bf16[4,3,64,512]{3,2,1,0:T(8,128)(2,1)S(1)}) custom-call(bf16[1024,512]{1,0:T(8,128)(2,1)S(1)} %get-tuple-element.29.keys, bf16[1024,512]{1,0:T(8,128)(2,1)S(1)} %get-tuple-element.30.values, bf16[3,512,512]{2,1,0:T(8,128)(2,1)S(1)} %shard_map.65.weights), custom_call_target="tpu_custom_call" | custom-call | flops 3221225472 | bytes 4194304 | tf_op jit(solution)/shard_map/pallas_call | solution.py:253
  235.4 4.7 %collective-permute-start.15 = (bf16[4,3,64,512]{3,2,1,0:T(8,128)(2,1)S(1)}, bf16[4,3,64,512]{3,2,1,0:T(8,128)(2,1)S(1)}, u32[]{:S(2)}, u32[]{:S(2)}) collective-permute-start(bf16[4,3,64,512]{3,2,1,0:T(8,128)(2,1)S(1)} %get-tuple-element.42), channel_id=1, source_target_pairs={{0,16},{16,0},{32,48},{48,32},{64,80},{80,64},{96,112},{112,96},{1... | collective-permute-start | bytes 2359304 | tf_op jit(solution)/shard_map/ppermute | solution.py:359
  240.1 1.9 collective-permute-done.15.recv
  242.7 2.2 collective-permute-start.18
  244.9 8.8 %collective-permute-done.16.one = bf16[3,64,512]{2,1,0:T(8,128)(2,1)S(1)} collective-permute-done((bf16[3,64,512]{2,1,0:T(8,128)(2,1)S(1)}, bf16[3,64,512]{2,1,0:T(8,128)(2,1)S(1)}, u32[]{:S(2)}, u32[]{:S(2)}) %collective-permute-start.16) | collective-permute-done | bytes 196640 | tf_op jit(solution)/shard_map/ppermute | solution.py:359
  254.6 4.7 %collective-permute-done.19.recv = bf16[3,64,512]{2,1,0:T(8,128)(2,1)S(1)} collective-permute-done((bf16[3,64,512]{2,1,0:T(8,128)(2,1)S(1)}, bf16[3,64,512]{2,1,0:T(8,128)(2,1)S(1)}, u32[]{:S(2)}, u32[]{:S(2)}) %collective-permute-start.19) | collective-permute-done | bytes 196640 | tf_op jit(solution)/shard_map/ppermute | solution.py:359
  259.3 1.0 shard_map.69
  260.3 1.9 collective-permute-start.20
  262.2 2.7 collective-permute-start.21
  264.9 2.2 collective-permute-start.23
  267.1 3.3 %collective-permute-start.24 = (bf16[3,64,512]{2,1,0:T(8,128)(2,1)S(1)}, bf16[3,64,512]{2,1,0:T(8,128)(2,1)S(1)}, u32[]{:S(2)}, u32[]{:S(2)}) collective-permute-start(bf16[3,64,512]{2,1,0:T(8,128)(2,1)S(1)} %collective-permute-done.20.refs_1_), channel_id=1, source_target_pairs={{0,16},{16,0},{32,48},{48,32},{64,80},{80,64},{96,112},{112,96},{1... | collective-permute-start | bytes 589832 | tf_op jit(solution)/shard_map/ppermute | solution.py:359
  270.5 2.0 collective-permute-done.21.refs_2_
  272.4 2.5 collective-permute-start.25
  275.0 0.7 slice_bitcast_fusion.2
  275.8 1.0 collective-permute-done.tails
  276.9 4.9 %shard_map.56 = (bf16[1024,512]{1,0:T(8,128)(2,1)S(1)}, bf16[1024,512]{1,0:T(8,128)(2,1)S(1)}) custom-call(bf16[16,2,64,512]{3,2,1,0:T(8,128)(2,1)} %all-to-all-done.source, bf16[2,8,512]{2,1,0:T(8,128)(2,1)S(1)} %collective-permute-done.tails, f32[3,4,8192]{2,1,0:T(4,128)S(1)} %copy-done, f32[2,1,512]{2,1,0:T(1,128)S(1)} %copy-done.1), custom_call_target="tpu_custom_call" | custom-call | bytes 8388608 | tf_op jit(solution)/shard_map/pallas_call | solution.py:213
  281.8 3.5 %shard_map.71.rest_0_ = bf16[2,1024,512]{2,1,0:T(8,128)(2,1)} custom-call(bf16[1024,512]{1,0:T(8,128)(2,1)S(1)} %get-tuple-element.50.queries, bf16[3,512,512]{2,1,0:T(8,128)(2,1)S(1)} %shard_map.65.weights), custom_call_target="tpu_custom_call" | custom-call | flops 1610612736 | bytes 4194304 | tf_op jit(solution)/shard_map/pallas_call | solution.py:346
  285.4 3.5 %shard_map.72 = bf16[2,1024,512]{2,1,0:T(8,128)(2,1)} custom-call(bf16[1024,512]{1,0:T(8,128)(2,1)S(1)} %get-tuple-element.28.queries, bf16[3,512,512]{2,1,0:T(8,128)(2,1)S(1)} %shard_map.70.weights, bf16[2,1024,512]{2,1,0:T(8,128)(2,1)} %shard_map.71.rest_0_), custom_call_target="tpu_custom_call", output_to_operand_aliasing={{}: (2, {})} | custom-call | flops 1610612736 | bytes 4194304 | tf_op jit(solution)/shard_map/pallas_call | solution.py:346
  (43 shorter events, 3.3 us)
Async XLA Ops:
  2.8 59.0 %all-to-all-start.2 = ((bf16[16,2,64,512]{3,2,1,0:T(8,128)(2,1)}), bf16[16,2,64,512]{3,2,1,0:T(8,128)(2,1)S(1)}, u32[]{:S(2)}, u32[]{:S(2)}) async-start(bf16[16,2,64,512]{3,2,1,0:T(8,128)(2,1)} %shard_map.58), calls=%async_computation.2 | async-start | bytes 4194304 | tf_op jit(solution)/shard_map/all_to_all | solution.py:376
  61.8 1.3 copy-start.3
  63.1 50.8 %all-to-all-start.1 = ((bf16[16,2,64,512]{3,2,1,0:T(8,128)(2,1)}), bf16[16,2,64,512]{3,2,1,0:T(8,128)(2,1)S(1)}, u32[]{:S(2)}, u32[]{:S(2)}) async-start(bf16[16,2,64,512]{3,2,1,0:T(8,128)(2,1)} %shard_map.57), calls=%async_computation.1 | async-start | bytes 4194304 | tf_op jit(solution)/shard_map/all_to_all | solution.py:376
  73.7 60.3 %copy-start = (f32[3,4,8192]{2,1,0:T(4,128)S(1)}, f32[3,4,8192]{2,1,0:T(4,128)}, u32[]{:S(2)}) copy-start(f32[3,4,8192]{2,1,0:T(4,128)} %taps.5) | copy-start | bytes 1179652
  73.7 60.3 %copy-start.1 = (f32[2,1,512]{2,1,0:T(1,128)S(1)}, f32[2,1,512]{2,1,0:T(1,128)}, u32[]{:S(2)}) copy-start(f32[2,1,512]{2,1,0:T(1,128)} %gain.5) | copy-start | bytes 12292
  113.9 1.4 copy-start.2
  115.3 159.7 %all-to-all-start = ((bf16[16,2,64,512]{3,2,1,0:T(8,128)(2,1)}), bf16[16,2,64,512]{3,2,1,0:T(8,128)(2,1)}, u32[]{:S(2)}, u32[]{:S(2)}) async-start(bf16[16,2,64,512]{3,2,1,0:T(8,128)(2,1)} %shard_map.55), calls=%async_computation | async-start | bytes 4194304 | tf_op jit(solution)/shard_map/all_to_all | solution.py:376
  127.7 6.4 %collective-permute-start.2 = (bf16[2,8,512]{2,1,0:T(8,128)(2,1)S(1)}, bf16[2,8,512]{2,1,0:T(8,128)(2,1)S(1)}, u32[]{:S(2)}, u32[]{:S(2)}) collective-permute-start(bf16[2,8,512]{2,1,0:T(8,128)(2,1)S(1)} %slice_bitcast_fusion), channel_id=1, source_target_pairs={{0,16},{16,32},{32,48},{48,64},{64,80},{80,96},{96,112},{112,128},... | collective-permute-start | bytes 49160 | tf_op jit(solution)/shard_map/ppermute | solution.py:359
  145.1 44.9 %collective-permute-start.3 = (bf16[4,3,64,512]{3,2,1,0:T(8,128)(2,1)S(1)}, bf16[4,3,64,512]{3,2,1,0:T(8,128)(2,1)S(1)}, u32[]{:S(2)}, u32[]{:S(2)}) collective-permute-start(bf16[4,3,64,512]{3,2,1,0:T(8,128)(2,1)S(1)} %get-tuple-element.35), channel_id=1, source_target_pairs={{0,16},{16,0},{32,48},{48,32},{64,80},{80,64},{96,112},{112,96},{1... | collective-permute-start | bytes 2359304 | tf_op jit(solution)/shard_map/ppermute | solution.py:359
  190.2 11.9 %collective-permute-start.4 = (bf16[3,64,512]{2,1,0:T(8,128)(2,1)S(1)}, bf16[3,64,512]{2,1,0:T(8,128)(2,1)S(1)}, u32[]{:S(2)}, u32[]{:S(2)}) collective-permute-start(bf16[3,64,512]{2,1,0:T(8,128)(2,1)S(1)} %get-tuple-element.37), channel_id=1, source_target_pairs={{0,32},{16,48},{32,64},{48,80},{64,96},{80,112},{96,0},{112,16},{1... | collective-permute-start | bytes 589832 | tf_op jit(solution)/shard_map/ppermute | solution.py:359
  190.3 11.8 %collective-permute-start.5 = (bf16[3,64,512]{2,1,0:T(8,128)(2,1)S(1)}, bf16[3,64,512]{2,1,0:T(8,128)(2,1)S(1)}, u32[]{:S(2)}, u32[]{:S(2)}) collective-permute-start(bf16[3,64,512]{2,1,0:T(8,128)(2,1)S(1)} %get-tuple-element.38), channel_id=1, source_target_pairs={{0,64},{16,80},{32,96},{48,112},{64,0},{80,16},{96,32},{112,48},{1... | collective-permute-start | bytes 589832 | tf_op jit(solution)/shard_map/ppermute | solution.py:359
  190.4 11.8 %collective-permute-start.6 = (bf16[3,64,512]{2,1,0:T(8,128)(2,1)S(1)}, bf16[3,64,512]{2,1,0:T(8,128)(2,1)S(1)}, u32[]{:S(2)}, u32[]{:S(2)}) collective-permute-start(bf16[3,64,512]{2,1,0:T(8,128)(2,1)S(1)} %get-tuple-element.39), channel_id=1, source_target_pairs={{0,96},{16,112},{32,0},{48,16},{64,32},{80,48},{96,64},{112,80},{1... | collective-permute-start | bytes 589832 | tf_op jit(solution)/shard_map/ppermute | solution.py:359
  202.3 5.1 %collective-permute-start.7 = (bf16[3,64,512]{2,1,0:T(8,128)(2,1)S(1)}, bf16[3,64,512]{2,1,0:T(8,128)(2,1)S(1)}, u32[]{:S(2)}, u32[]{:S(2)}) collective-permute-start(bf16[3,64,512]{2,1,0:T(8,128)(2,1)S(1)} %shard_map.63.mine), channel_id=1, source_target_pairs={{0,128},{16,144},{32,160},{48,176},{64,192},{80,208},{96,224},{112... | collective-permute-start | bytes 589832 | tf_op jit(solution)/shard_map/ppermute | solution.py:359
  207.5 6.9 %collective-permute-start.8 = (bf16[3,64,512]{2,1,0:T(8,128)(2,1)S(1)}, bf16[3,64,512]{2,1,0:T(8,128)(2,1)S(1)}, u32[]{:S(2)}, u32[]{:S(2)}) collective-permute-start(bf16[3,64,512]{2,1,0:T(8,128)(2,1)S(1)} %get-tuple-element.40.refs_0_), channel_id=1, source_target_pairs={{0,32},{16,48},{32,64},{48,80},{64,96},{80,112},{96,0},{112,16},{1... | collective-permute-start | bytes 589832 | tf_op jit(solution)/shard_map/ppermute | solution.py:359
  209.5 10.3 %collective-permute-start.9 = (bf16[3,64,512]{2,1,0:T(8,128)(2,1)S(1)}, bf16[3,64,512]{2,1,0:T(8,128)(2,1)S(1)}, u32[]{:S(2)}, u32[]{:S(2)}) collective-permute-start(bf16[3,64,512]{2,1,0:T(8,128)(2,1)S(1)} %get-tuple-element.40.refs_0_), channel_id=1, source_target_pairs={{0,64},{16,80},{32,96},{48,112},{64,0},{80,16},{96,32},{112,48},{1... | collective-permute-start | bytes 589832 | tf_op jit(solution)/shard_map/ppermute | solution.py:359
  212.2 10.1 %collective-permute-start.10 = (bf16[3,64,512]{2,1,0:T(8,128)(2,1)S(1)}, bf16[3,64,512]{2,1,0:T(8,128)(2,1)S(1)}, u32[]{:S(2)}, u32[]{:S(2)}) collective-permute-start(bf16[3,64,512]{2,1,0:T(8,128)(2,1)S(1)} %get-tuple-element.40.refs_0_), channel_id=1, source_target_pairs={{0,96},{16,112},{32,0},{48,16},{64,32},{80,48},{96,64},{112,80},{1... | collective-permute-start | bytes 589832 | tf_op jit(solution)/shard_map/ppermute | solution.py:359
  212.2 17.4 %collective-permute-start.11 = (bf16[3,64,512]{2,1,0:T(8,128)(2,1)S(1)}, bf16[3,64,512]{2,1,0:T(8,128)(2,1)S(1)}, u32[]{:S(2)}, u32[]{:S(2)}) collective-permute-start(bf16[3,64,512]{2,1,0:T(8,128)(2,1)S(1)} %get-tuple-element.40.refs_0_), channel_id=1, source_target_pairs={{0,16},{16,0},{32,48},{48,32},{64,80},{80,64},{96,112},{112,96},{1... | collective-permute-start | bytes 589832 | tf_op jit(solution)/shard_map/ppermute | solution.py:359
  214.5 15.1 %collective-permute-start.12 = (bf16[3,64,512]{2,1,0:T(8,128)(2,1)S(1)}, bf16[3,64,512]{2,1,0:T(8,128)(2,1)S(1)}, u32[]{:S(2)}, u32[]{:S(2)}) collective-permute-start(bf16[3,64,512]{2,1,0:T(8,128)(2,1)S(1)} %collective-permute-done.8.refs_1_), channel_id=1, source_target_pairs={{0,16},{16,0},{32,48},{48,32},{64,80},{80,64},{96,112},{112,96},{1... | collective-permute-start | bytes 589832 | tf_op jit(solution)/shard_map/ppermute | solution.py:359
  219.8 9.8 %collective-permute-start.13 = (bf16[3,64,512]{2,1,0:T(8,128)(2,1)S(1)}, bf16[3,64,512]{2,1,0:T(8,128)(2,1)S(1)}, u32[]{:S(2)}, u32[]{:S(2)}) collective-permute-start(bf16[3,64,512]{2,1,0:T(8,128)(2,1)S(1)} %collective-permute-done.9.refs_2_), channel_id=1, source_target_pairs={{0,16},{16,0},{32,48},{48,32},{64,80},{80,64},{96,112},{112,96},{1... | collective-permute-start | bytes 589832 | tf_op jit(solution)/shard_map/ppermute | solution.py:359
  222.3 7.3 %collective-permute-start.14 = (bf16[3,64,512]{2,1,0:T(8,128)(2,1)S(1)}, bf16[3,64,512]{2,1,0:T(8,128)(2,1)S(1)}, u32[]{:S(2)}, u32[]{:S(2)}) collective-permute-start(bf16[3,64,512]{2,1,0:T(8,128)(2,1)S(1)} %collective-permute-done.10.refs_3_), channel_id=1, source_target_pairs={{0,16},{16,0},{32,48},{48,32},{64,80},{80,64},{96,112},{112,96},{1... | collective-permute-start | bytes 589832 | tf_op jit(solution)/shard_map/ppermute | solution.py:359
  223.0 1.2 collective-permute-start.1
  235.4 6.6 %collective-permute-start.15 = (bf16[4,3,64,512]{3,2,1,0:T(8,128)(2,1)S(1)}, bf16[4,3,64,512]{3,2,1,0:T(8,128)(2,1)S(1)}, u32[]{:S(2)}, u32[]{:S(2)}) collective-permute-start(bf16[4,3,64,512]{3,2,1,0:T(8,128)(2,1)S(1)} %get-tuple-element.42), channel_id=1, source_target_pairs={{0,16},{16,0},{32,48},{48,32},{64,80},{80,64},{96,112},{112,96},{1... | collective-permute-start | bytes 2359304 | tf_op jit(solution)/shard_map/ppermute | solution.py:359
  242.2 11.6 %collective-permute-start.16 = (bf16[3,64,512]{2,1,0:T(8,128)(2,1)S(1)}, bf16[3,64,512]{2,1,0:T(8,128)(2,1)S(1)}, u32[]{:S(2)}, u32[]{:S(2)}) collective-permute-start(bf16[3,64,512]{2,1,0:T(8,128)(2,1)S(1)} %get-tuple-element.44), channel_id=1, source_target_pairs={{0,32},{16,48},{32,64},{48,80},{64,96},{80,112},{96,0},{112,16},{1... | collective-permute-start | bytes 589832 | tf_op jit(solution)/shard_map/ppermute | solution.py:359
  242.2 11.5 %collective-permute-start.17 = (bf16[3,64,512]{2,1,0:T(8,128)(2,1)S(1)}, bf16[3,64,512]{2,1,0:T(8,128)(2,1)S(1)}, u32[]{:S(2)}, u32[]{:S(2)}) collective-permute-start(bf16[3,64,512]{2,1,0:T(8,128)(2,1)S(1)} %get-tuple-element.45), channel_id=1, source_target_pairs={{0,64},{16,80},{32,96},{48,112},{64,0},{80,16},{96,32},{112,48},{1... | collective-permute-start | bytes 589832 | tf_op jit(solution)/shard_map/ppermute | solution.py:359
  242.7 11.4 %collective-permute-start.18 = (bf16[3,64,512]{2,1,0:T(8,128)(2,1)S(1)}, bf16[3,64,512]{2,1,0:T(8,128)(2,1)S(1)}, u32[]{:S(2)}, u32[]{:S(2)}) collective-permute-start(bf16[3,64,512]{2,1,0:T(8,128)(2,1)S(1)} %get-tuple-element.46), channel_id=1, source_target_pairs={{0,96},{16,112},{32,0},{48,16},{64,32},{80,48},{96,64},{112,80},{1... | collective-permute-start | bytes 589832 | tf_op jit(solution)/shard_map/ppermute | solution.py:359
  254.2 5.1 %collective-permute-start.19 = (bf16[3,64,512]{2,1,0:T(8,128)(2,1)S(1)}, bf16[3,64,512]{2,1,0:T(8,128)(2,1)S(1)}, u32[]{:S(2)}, u32[]{:S(2)}) collective-permute-start(bf16[3,64,512]{2,1,0:T(8,128)(2,1)S(1)} %shard_map.68.mine), channel_id=1, source_target_pairs={{0,128},{16,144},{32,160},{48,176},{64,192},{80,208},{96,224},{112... | collective-permute-start | bytes 589832 | tf_op jit(solution)/shard_map/ppermute | solution.py:359
  260.3 6.9 %collective-permute-start.20 = (bf16[3,64,512]{2,1,0:T(8,128)(2,1)S(1)}, bf16[3,64,512]{2,1,0:T(8,128)(2,1)S(1)}, u32[]{:S(2)}, u32[]{:S(2)}) collective-permute-start(bf16[3,64,512]{2,1,0:T(8,128)(2,1)S(1)} %get-tuple-element.49.refs_0_), channel_id=1, source_target_pairs={{0,32},{16,48},{32,64},{48,80},{64,96},{80,112},{96,0},{112,16},{1... | collective-permute-start | bytes 589832 | tf_op jit(solution)/shard_map/ppermute | solution.py:359
  262.2 10.3 %collective-permute-start.21 = (bf16[3,64,512]{2,1,0:T(8,128)(2,1)S(1)}, bf16[3,64,512]{2,1,0:T(8,128)(2,1)S(1)}, u32[]{:S(2)}, u32[]{:S(2)}) collective-permute-start(bf16[3,64,512]{2,1,0:T(8,128)(2,1)S(1)} %get-tuple-element.49.refs_0_), channel_id=1, source_target_pairs={{0,64},{16,80},{32,96},{48,112},{64,0},{80,16},{96,32},{112,48},{1... | collective-permute-start | bytes 589832 | tf_op jit(solution)/shard_map/ppermute | solution.py:359
  264.9 10.1 %collective-permute-start.22 = (bf16[3,64,512]{2,1,0:T(8,128)(2,1)S(1)}, bf16[3,64,512]{2,1,0:T(8,128)(2,1)S(1)}, u32[]{:S(2)}, u32[]{:S(2)}) collective-permute-start(bf16[3,64,512]{2,1,0:T(8,128)(2,1)S(1)} %get-tuple-element.49.refs_0_), channel_id=1, source_target_pairs={{0,96},{16,112},{32,0},{48,16},{64,32},{80,48},{96,64},{112,80},{1... | collective-permute-start | bytes 589832 | tf_op jit(solution)/shard_map/ppermute | solution.py:359
  264.9 20.4 %collective-permute-start.23 = (bf16[3,64,512]{2,1,0:T(8,128)(2,1)S(1)}, bf16[3,64,512]{2,1,0:T(8,128)(2,1)S(1)}, u32[]{:S(2)}, u32[]{:S(2)}) collective-permute-start(bf16[3,64,512]{2,1,0:T(8,128)(2,1)S(1)} %get-tuple-element.49.refs_0_), channel_id=1, source_target_pairs={{0,16},{16,0},{32,48},{48,32},{64,80},{80,64},{96,112},{112,96},{1... | collective-permute-start | bytes 589832 | tf_op jit(solution)/shard_map/ppermute | solution.py:359
  267.1 18.2 %collective-permute-start.24 = (bf16[3,64,512]{2,1,0:T(8,128)(2,1)S(1)}, bf16[3,64,512]{2,1,0:T(8,128)(2,1)S(1)}, u32[]{:S(2)}, u32[]{:S(2)}) collective-permute-start(bf16[3,64,512]{2,1,0:T(8,128)(2,1)S(1)} %collective-permute-done.20.refs_1_), channel_id=1, source_target_pairs={{0,16},{16,0},{32,48},{48,32},{64,80},{80,64},{96,112},{112,96},{1... | collective-permute-start | bytes 589832 | tf_op jit(solution)/shard_map/ppermute | solution.py:359
  272.4 12.9 %collective-permute-start.25 = (bf16[3,64,512]{2,1,0:T(8,128)(2,1)S(1)}, bf16[3,64,512]{2,1,0:T(8,128)(2,1)S(1)}, u32[]{:S(2)}, u32[]{:S(2)}) collective-permute-start(bf16[3,64,512]{2,1,0:T(8,128)(2,1)S(1)} %collective-permute-done.21.refs_2_), channel_id=1, source_target_pairs={{0,16},{16,0},{32,48},{48,32},{64,80},{80,64},{96,112},{112,96},{1... | collective-permute-start | bytes 589832 | tf_op jit(solution)/shard_map/ppermute | solution.py:359
  274.9 10.4 %collective-permute-start.26 = (bf16[3,64,512]{2,1,0:T(8,128)(2,1)S(1)}, bf16[3,64,512]{2,1,0:T(8,128)(2,1)S(1)}, u32[]{:S(2)}, u32[]{:S(2)}) collective-permute-start(bf16[3,64,512]{2,1,0:T(8,128)(2,1)S(1)} %collective-permute-done.22.refs_3_), channel_id=1, source_target_pairs={{0,16},{16,0},{32,48},{48,32},{64,80},{80,64},{96,112},{112,96},{1... | collective-permute-start | bytes 589832 | tf_op jit(solution)/shard_map/ppermute | solution.py:359
  275.7 1.2 collective-permute-start

commit v3 on v2

--- a/solution.py
+++ b/solution.py
@@ -79,12 +79,14 @@
     return taps[stream, :, cols]
 
 
-def edge_rows(first, tails, earlier, stream):
+def edge_rows(tails, stream, group):
+    def taken(at):
+        return sum(part[stream, at].astype(F32) for part in tails)
+
     later = lax.axis_index("seq") > 0
-    here = tails[stream].astype(F32)
-    if first:
-        return jnp.where(later, here, jnp.zeros_like(here))
-    return jnp.where(later, here, earlier[stream].astype(F32))
+    here = taken(group)
+    before = jnp.zeros_like(here) if group == 0 else taken(group - 1)
+    return jnp.where(later, here, before)
 
 
 def conv_chunk(raw, stream, n, edge, taps):
@@ -116,44 +118,11 @@
     return pltpu.with_memory_space_constraint(value, pltpu.HBM)
 
 
-def spread(source, spots):
-    def body(source, out, stage, sems_in, sems_out):
-        def pull(s, h):
-            stream, group = spots[s]
-            cols = pl.ds(h * HEAD, HEAD)
-            return pltpu.make_async_copy(
-                source.at[stream, group, :, cols], stage.at[h, s], sems_in.at[s, h]
-            )
-
-        def push(s, h):
-            return pltpu.make_async_copy(stage.at[h, s], out.at[h, s], sems_out.at[s, h])
-
-        both = [(s, h) for s in range(2) for h in range(16)]
-        for spot in both:
-            pull(*spot).start()
-        for spot in both:
-            pull(*spot).wait()
-            push(*spot).start()
-        for spot in both:
-            push(*spot).wait()
-
-    return call(
-        body,
-        sds((16, 2, 64, HEAD), BF),
-        [hbm()],
-        [
-            pltpu.VMEM((16, 2, 64, HEAD), BF),
-            pltpu.SemaphoreType.DMA((2, 16)),
-            pltpu.SemaphoreType.DMA((2, 16)),
-        ],
-        nbytes=4 << 20,
-        out_specs=hbm(),
-        limit=60,
-    )(in_hbm(source))
-
-
-def prepare(first, source, tails, earlier, taps, gain, start):
-    def body(source, tails, earlier, taps, gain, *rest):
+def prepare(group, source, tails, taps, gain, start):
+    first = start is not None
+
+    def body(source, *rest):
+        tails, (taps, gain, *rest) = rest[:4], rest[4:]
         if first:
             start, keys, values, narrow, raw, sems, wide, wide_sem = rest
         else:
@@ -165,8 +134,8 @@
             fetch = pltpu.make_async_copy(start, wide, wide_sem)
             fetch.start()
         key_taps, value_taps = own_taps(taps, 1), own_taps(taps, 2)
-        key_edge = edge_rows(first, tails, earlier, 0)
-        value_edge = edge_rows(first, tails, earlier, 1)
+        key_edge = edge_rows(tails, 1, group)
+        value_edge = edge_rows(tails, 2, group)
 
         def step(n, carry):
             rows = chunk_rows(n)
@@ -186,20 +155,21 @@
     square = (3, HEAD, HEAD)
     outs = [rows, rows] + ([sds(square, BF)] if first else [])
     scratch = raw_scratch(2) + ([pltpu.VMEM(square, F32), pltpu.SemaphoreType.DMA(())] if first else [])
-    ins = [in_hbm(source), tails, earlier, taps, gain] + ([in_hbm(start)] if first else [])
-    specs = [hbm()] + [vmem()] * 4 + ([hbm()] if first else [])
+    ins = [in_hbm(source), *tails, taps, gain] + ([in_hbm(start)] if first else [])
+    specs = [hbm()] + [vmem()] * 6 + ([hbm()] if first else [])
     return call(body, outs, specs, scratch, nbytes=8 << 20, limit=24)(*ins)
 
 
 def prepare_queries(source, tails, taps, gain):
-    def body(source, tails, taps, gain, *rest):
+    def body(source, *rest):
+        tails, (taps, gain, *rest) = rest[:4], rest[4:]
         raw, sems = rest[-2:]
         for group in range(GROUPS):
             for n in range(BLOCKS):
                 raw_copy(source, raw, sems, 0, group, n).start()
         query_taps = own_taps(taps, 0)
         for group, queries in enumerate(rest[:GROUPS]):
-            edge = edge_rows(group == 0, tails.at[group : group + 1], tails, 0)
+            edge = edge_rows(tails, 0, group)
 
             def step(n, carry, group=group, queries=queries, edge=edge):
                 raw_copy(source, raw, sems, 0, group, n).wait()
@@ -211,8 +181,8 @@
 
     rows = sds((ROWS, HEAD), BF)
     return call(
-        body, [rows, rows], [hbm()] + [vmem()] * 3, raw_scratch(GROUPS), nbytes=8 << 20
-    )(in_hbm(source), tails, taps, gain)
+        body, [rows, rows], [hbm()] + [vmem()] * 6, raw_scratch(GROUPS), nbytes=8 << 20
+    )(in_hbm(source), *tails, taps, gain)
 
 
 def gradients(keys, values, weights, plain):
@@ -372,12 +342,114 @@
 
 
 def regroup(qkv_proj, spots):
-    ready = spread(qkv_proj, spots)
+    def by_head(sources, dests):
+        return [(pair_at(sources[0], spots, h * HEAD), dests[0].at[h]) for h in range(16)]
+
+    (ready,) = move([qkv_proj], [sds((16, 2, 64, HEAD), BF)], (16, 2, 64, HEAD), by_head)
     return lax.all_to_all(ready, "wide", 0, 0, tiled=True)
 
 
-def tails_behind(raw):
-    return seq_permute(raw[15, :, 56:64, :], lambda i: (i + 1) % 16)
+def move(ins, outs, stages, moves):
+    def body(*refs):
+        sources, dests = refs[: len(ins)], refs[len(ins) : len(ins) + len(outs)]
+        stage, sems_in, sems_out = refs[len(ins) + len(outs) :]
+        jobs = moves(sources, dests)
+
+        def pull(n):
+            return pltpu.make_async_copy(jobs[n][0], stage.at[n], sems_in.at[n])
+
+        def push(n):
+            return pltpu.make_async_copy(stage.at[n], jobs[n][1], sems_out.at[n])
+
+        for n in range(len(jobs)):
+            pull(n).start()
+        for n in range(len(jobs)):
+            pull(n).wait()
+            push(n).start()
+
+        def settle(n, carry):
+            pltpu.make_async_copy(stage.at[n], stage.at[n], sems_out.at[n]).wait()
+            return carry
+
+        lax.fori_loop(0, len(jobs), settle, 0)
+
+    return call(
+        body,
+        outs,
+        [hbm()] * len(ins),
+        [pltpu.VMEM(stages, BF), pltpu.SemaphoreType.DMA(stages[:1]), pltpu.SemaphoreType.DMA(stages[:1])],
+        nbytes=4 << 20,
+        out_specs=jax.tree.map(lambda _: hbm(), outs),
+        limit=60,
+    )(*[in_hbm(value) for value in ins])
+
+
+def wide_spot():
+    wide = lax.axis_index("wide")
+    return wide >> 2, wide & 3
+
+
+def pair_at(source, spots, cols):
+    (stream, group), (_, last) = spots
+    if group == last:
+        return source.at[pl.ds(stream, 2), group, :, pl.ds(cols, HEAD)]
+    return source.at[stream, pl.ds(group, 2), :, pl.ds(cols, HEAD)]
+
+
+def two_steps(qkv_proj, spots):
+    block = sds((4, 2, 64, HEAD), BF)
+
+    def by_x(sources, dests):
+        x, _ = wide_spot()
+        jobs = []
+        for k in range(4):
+            for z in range(4):
+                cols = pl.multiple_of(((x + k & 3) * 4 + z) * HEAD, HEAD)
+                jobs.append((pair_at(sources[0], spots, cols), dests[k].at[z]))
+        return jobs
+
+    def by_z(sources, dests):
+        _, z = wide_spot()
+        return [(sources[k].at[z + j & 3], dests[j].at[k]) for j in range(4) for k in range(4)]
+
+    def by_source(sources, dests):
+        x, z = wide_spot()
+        return [
+            (sources[j].at[k], dests[0].at[(x + 4 - k & 3) * 4 + (z + 4 - j & 3)])
+            for j in range(4)
+            for k in range(4)
+        ]
+
+    parts = move([qkv_proj], [block] * 4, (16, 2, 64, HEAD), by_x)
+    parts = [parts[0]] + [wide_shift(parts[d], d, 0) for d in (1, 3, 2)]
+    parts = [parts[0], parts[1], parts[3], parts[2]]
+    parts = move(parts, [block] * 4, (16, 2, 64, HEAD), by_z)
+    parts = [parts[0]] + [wide_shift(parts[d], 0, d) for d in (1, 3, 2)]
+    parts = [parts[0], parts[1], parts[3], parts[2]]
+    whole = move(parts, [sds((16, 2, 64, HEAD), BF)], (16, 2, 64, HEAD), by_source)
+    return whole[0]
+
+
+def wide_shift(value, dx, dz):
+    pairs = [(w, ((w >> 2) + dx & 3) * 4 + ((w & 3) + dz & 3)) for w in range(16)]
+    return lax.ppermute(value, "wide", pairs)
+
+
+def tails_behind(qkv_proj):
+    width = 4 * HEAD
+    pieces = [qkv_proj[:, :, 56:64, x * width : x * width + width] for x in range(4)]
+    x, _ = wide_spot()
+    found = jnp.where(x == 3, pieces[3], jnp.zeros_like(pieces[3]))
+    for d in range(3):
+        found = found + lax.ppermute(pieces[d], "wide", [(15, 4 * d + 3)])
+    parts = []
+    for t in range(4):
+        pairs = [
+            (s * 16 + 4 * at + 3, (s + 1) % 16 * 16 + 4 * at + t) for s in range(16) for at in range(4)
+        ]
+        piece = found[..., t * HEAD : t * HEAD + HEAD]
+        parts.append(lax.ppermute(piece, ("seq", "wide"), pairs))
+    return parts
 
 
 def reduce_pieces(keep, send):
@@ -403,21 +475,21 @@
     state = jnp.swapaxes(lax.dynamic_slice_in_dim(start, own_at, 64, 2), 1, 2)
 
     kv0 = regroup(qkv_proj, ((1, 0), (2, 0)))
-    tails0 = tails_behind(kv0)
-    kv1 = regroup(qkv_proj, ((1, 1), (2, 1)))
-    tails1 = tails_behind(kv1)
-    q = regroup(qkv_proj, ((0, 0), (0, 1)))
-    qtails = tails_behind(q)
-
-    keys, values, narrow = prepare(True, kv0, tails0, tails0, conv_kernel, qk_gain, start)
-    mine, recv = reduce_pieces(*gradients(keys, values, narrow, True))
+    tails = tails_behind(qkv_proj)
+    kv1 = two_steps(qkv_proj, ((1, 1), (2, 1)))
+    q = two_steps(qkv_proj, ((0, 0), (0, 1)))
+
+    keys, values, narrow = prepare(0, kv0, tails, conv_kernel, qk_gain, start)
+    keep, send = gradients(keys, values, narrow, True)
+    mine, recv = reduce_pieces(keep, send)
     moment, state, narrow = update(step_size, mine, recv, state, None)
     weights1 = assemble(gather_pieces(narrow))
-    keys, values = prepare(False, kv1, tails1, tails0, conv_kernel, qk_gain, None)
-    mine, recv = reduce_pieces(*gradients(keys, values, weights1, False))
+    keys, values = prepare(1, kv1, tails, conv_kernel, qk_gain, None)
+    keep, send = gradients(keys, values, weights1, False)
+    mine, recv = reduce_pieces(keep, send)
     moment, state, narrow = update(step_size, mine, recv, state, moment)
     weights2 = assemble(gather_pieces(narrow))
-    queries0, queries1 = prepare_queries(q, qtails, conv_kernel, qk_gain)
+    queries0, queries1 = prepare_queries(q, tails, conv_kernel, qk_gain)
     out = apply_fast(queries0, weights1, 0, None)
     return apply_fast(queries1, weights2, 1, out)
 

time: 295 us -> 317 us (1.075); the launches traced: 289 us -> 316 us
  waiting for transfers between devices: 121 us -> 163 us
  starting transfers between devices: 116 us -> 88 us
  Pallas kernels: 44.2 us -> 55.4 us
    ppermute x0 -> x19, waiting for transfers between devices: none -> 88.6 us  [the longest x12 45.3 us: wide_shift(): return lax.ppermute(value, 'wide', pairs)]
    all_to_all x3 -> x1, waiting for transfers between devices: 84.8 us -> 0.01 us  [regroup(): return lax.all_to_all(ready, 'wide', 0, 0, tiled=True)]
    ppermute x27 -> x24, waiting for transfers between devices: 36.5 us -> 74 us  [seq_permute(): return lax.ppermute(value, 'seq', [(i, target(i)) for i in range(16)])]
    ppermute x27 -> x24, starting transfers between devices: 84.9 us -> 55.3 us  [seq_permute(): return lax.ppermute(value, 'seq', [(i, target(i)) for i in range(16)])]
    ppermute x0 -> x19, starting transfers between devices: none -> 21.1 us  [the longest x12 15.1 us: wide_shift(): return lax.ppermute(value, 'wide', pairs)]
    all_to_all x3 -> x1, starting transfers between devices: 31 us -> 11.6 us  [regroup(): return lax.all_to_all(ready, 'wide', 0, 0, tiled=True)]
    pallas_call x4 -> x8, Pallas kernels: 13.3 us -> 23.1 us  [the longest x7 18.2 us: move(): call(body, outs, [hbm()] * len(ins), [pltpu.VMEM(stages, BF), pltpu.Semap...]
  transfers between devices with their start and end apart: 30 -> 44, of which waited for: 14 -> 15; matrix products, arithmetic and copies ran while one was open for 1% -> 1% of each run, Pallas kernels for 13% -> 10%
where the time goes in v3:
time: 317 us; the launch traced here: 316 us
  waiting for transfers between devices  163 us (51%)
  starting transfers between devices  88 us (28%)
  Pallas kernels  55.4 us (17%)
  local copies, waits for them, and re-layouts  7.65 us (2%)
    ppermute x24, waiting for transfers between devices, seq_permute(): return lax.ppermute(value, 'seq', [(i, target(i)) for i in range(16)])  74 us
    ppermute x24, starting transfers between devices, seq_permute(): return lax.ppermute(value, 'seq', [(i, target(i)) for i in range(16)])  55.3 us
    ppermute x12, waiting for transfers between devices, wide_shift(): return lax.ppermute(value, 'wide', pairs)  45.3 us
    ppermute x4, waiting for transfers between devices, tails_behind(): parts.append(lax.ppermute(piece, ('seq', 'wide'), pairs))  43.3 us
    pallas_call x7, Pallas kernels, move(): call(body, outs, [hbm()] * len(ins), [pltpu.VMEM(stages, BF), pltpu.Semap...  18.2 us
    ppermute x12, starting transfers between devices, wide_shift(): return lax.ppermute(value, 'wide', pairs)  15.1 us
    pallas_call x2, Pallas kernels, gradients(): call(body, [half, half], [vmem()] * 3, [pltpu.VMEM((ROWS, HEAD), BF)] * 3...  12.4 us
    all_to_all x1, starting transfers between devices, regroup(): return lax.all_to_all(ready, 'wide', 0, 0, tiled=True)  11.6 us
  transfers between devices with their start and end apart: 44, of which 15 were waited for; matrix products, arithmetic and copies ran while one was open for 1% of the time, Pallas kernels for 10%

profile of v3, /device:TPU:1, one launch (start us, length us, event | category | flops | bytes accessed | tf_op | source)
XLA Modules:
  0.0 316.1 jit_solution(16923326996585761241)
XLA Ops:
  0.0 2.6 shard_map.63
  2.6 11.6 %all-to-all-start = ((bf16[16,2,64,512]{3,2,1,0:T(8,128)(2,1)}), bf16[16,2,64,512]{3,2,1,0:T(8,128)(2,1)S(1)}, u32[]{:S(2)}, u32[]{:S(2)}) async-start(bf16[16,2,64,512]{3,2,1,0:T(8,128)(2,1)} %shard_map.63), calls=%async_computation | async-start | bytes 4194304 | tf_op jit(solution)/shard_map/all_to_all | solution.py:349
  16.8 1.4 collective-permute-start.7
  21.3 1.3 collective-permute-start.9
  22.6 43.3 %collective-permute-done.9.rest_0_ = bf16[3,2,8,512]{3,2,1,0:T(8,128)(2,1)S(1)} collective-permute-done((bf16[3,2,8,512]{3,2,1,0:T(8,128)(2,1)S(1)}, bf16[3,2,8,512]{3,2,1,0:T(8,128)(2,1)S(1)}, u32[]{:S(2)}, u32[]{:S(2)}) %collective-permute-start.9) | collective-permute-done | bytes 49184 | tf_op jit(solution)/shard_map/ppermute | solution.py:451
  65.9 1.3 copy-done.14
  67.2 5.6 %shard_map.64 = (bf16[1024,512]{1,0:T(8,128)(2,1)S(1)}, bf16[1024,512]{1,0:T(8,128)(2,1)S(1)}, bf16[3,512,512]{2,1,0:T(8,128)(2,1)S(1)}) custom-call(bf16[16,2,64,512]{3,2,1,0:T(8,128)(2,1)} %copy-done.14, bf16[3,2,8,512]{3,2,1,0:T(8,128)(2,1)S(1)} %collective-permute-done.9.rest_0_, bf16[3,2,8,512]{3,2,1,0:T(8,128)(2,1)S(1)} %collective-permute-done.10.rest_1_, ...), custom_call_target="tpu_custom_call" | custom-call | bytes 8388608 | tf_op jit(solution)/shard_map/pallas_call | solution.py:160
  72.8 6.2 %shard_map.65 = (bf16[4,3,64,512]{3,2,1,0:T(8,128)(2,1)S(1)}, bf16[4,3,64,512]{3,2,1,0:T(8,128)(2,1)}) custom-call(bf16[1024,512]{1,0:T(8,128)(2,1)S(1)} %get-tuple-element.63.keys, bf16[1024,512]{1,0:T(8,128)(2,1)S(1)} %get-tuple-element.64.values, bf16[3,512,512]{2,1,0:T(8,128)(2,1)S(1)} %get-tuple-element.65.weights), custom_call_target="tpu_custom_call" | custom-call | flops 3221225472 | bytes 4194304 | tf_op jit(solution)/shard_map/pallas_call | solution.py:223
  79.0 3.7 %collective-permute-start.19 = (bf16[4,3,64,512]{3,2,1,0:T(8,128)(2,1)}, bf16[4,3,64,512]{3,2,1,0:T(8,128)(2,1)S(1)}, u32[]{:S(2)}, u32[]{:S(2)}) collective-permute-start(bf16[4,3,64,512]{3,2,1,0:T(8,128)(2,1)} %get-tuple-element.67), channel_id=1, source_target_pairs={{0,16},{16,0},{32,48},{48,32},{64,80},{80,64},{96,112},{112,96},{1... | collective-permute-start | bytes 2359304 | tf_op jit(solution)/shard_map/ppermute | solution.py:329
  82.7 2.7 shard_map.59
  86.6 2.4 collective-permute-start.14
  90.2 10.1 %collective-permute-done.13.refs_1_ = bf16[4,2,64,512]{3,2,1,0:T(8,128)(2,1)S(1)} collective-permute-done((bf16[4,2,64,512]{3,2,1,0:T(8,128)(2,1)}, bf16[4,2,64,512]{3,2,1,0:T(8,128)(2,1)S(1)}, u32[]{:S(2)}, u32[]{:S(2)}) %collective-permute-start.13) | collective-permute-done | bytes 524320 | tf_op jit(solution)/shard_map/ppermute | solution.py:435
  100.3 12.1 %collective-permute-done.14.refs_2_ = bf16[4,2,64,512]{3,2,1,0:T(8,128)(2,1)S(1)} collective-permute-done((bf16[4,2,64,512]{3,2,1,0:T(8,128)(2,1)}, bf16[4,2,64,512]{3,2,1,0:T(8,128)(2,1)S(1)}, u32[]{:S(2)}, u32[]{:S(2)}) %collective-permute-start.14) | collective-permute-done | bytes 524320 | tf_op jit(solution)/shard_map/ppermute | solution.py:435
  113.4 2.6 shard_map.60
  116.8 2.8 collective-permute-start.21
  120.8 2.6 collective-permute-done.20.one
  123.4 4.1 %collective-permute-done.21.two = bf16[3,64,512]{2,1,0:T(8,128)(2,1)S(1)} collective-permute-done((bf16[3,64,512]{2,1,0:T(8,128)(2,1)S(1)}, bf16[3,64,512]{2,1,0:T(8,128)(2,1)S(1)}, u32[]{:S(2)}, u32[]{:S(2)}) %collective-permute-start.21) | collective-permute-done | bytes 196640 | tf_op jit(solution)/shard_map/ppermute | solution.py:329
  127.9 2.8 collective-permute-start.23
  132.4 1.4 constant_dynamic-slice_fusion
  134.1 31.0 %collective-permute-done.23.recv = bf16[3,64,512]{2,1,0:T(8,128)(2,1)S(1)} collective-permute-done((bf16[3,64,512]{2,1,0:T(8,128)(2,1)S(1)}, bf16[3,64,512]{2,1,0:T(8,128)(2,1)S(1)}, u32[]{:S(2)}, u32[]{:S(2)}) %collective-permute-start.23) | collective-permute-done | bytes 196640 | tf_op jit(solution)/shard_map/ppermute | solution.py:329
  165.2 1.8 collective-permute-start.26
  167.9 2.7 collective-permute-start.27
  170.7 5.7 %collective-permute-start.30 = (bf16[3,64,512]{2,1,0:T(8,128)(2,1)S(1)}, bf16[3,64,512]{2,1,0:T(8,128)(2,1)S(1)}, u32[]{:S(2)}, u32[]{:S(2)}) collective-permute-start(bf16[3,64,512]{2,1,0:T(8,128)(2,1)S(1)} %collective-permute-done.26.refs_3_), channel_id=1, source_target_pairs={{0,16},{16,0},{32,48},{48,32},{64,80},{80,64},{96,112},{112,96},{1... | collective-permute-start | bytes 589832 | tf_op jit(solution)/shard_map/ppermute | solution.py:329
  176.4 1.6 collective-permute-start.29
  180.0 2.6 shard_map.61.source
  182.6 5.4 %shard_map.62 = (bf16[1024,512]{1,0:T(8,128)(2,1)S(1)}, bf16[1024,512]{1,0:T(8,128)(2,1)S(1)}) custom-call(bf16[16,2,64,512]{3,2,1,0:T(8,128)(2,1)} %shard_map.61.source, bf16[3,2,8,512]{3,2,1,0:T(8,128)(2,1)S(1)} %collective-permute-done.9.rest_0_, bf16[3,2,8,512]{3,2,1,0:T(8,128)(2,1)S(1)} %collective-permute-done.10.rest_1_, ...), custom_call_target="tpu_custom_call" | custom-call | bytes 8388608 | tf_op jit(solution)/shard_map/pallas_call | solution.py:160
  189.8 6.3 %shard_map.70 = (bf16[4,3,64,512]{3,2,1,0:T(8,128)(2,1)S(1)}, bf16[4,3,64,512]{3,2,1,0:T(8,128)(2,1)}) custom-call(bf16[1024,512]{1,0:T(8,128)(2,1)S(1)} %get-tuple-element.61.keys, bf16[1024,512]{1,0:T(8,128)(2,1)S(1)} %get-tuple-element.62.values, bf16[3,512,512]{2,1,0:T(8,128)(2,1)S(1)} %shard_map.69.weights), custom_call_target="tpu_custom_call" | custom-call | flops 3221225472 | bytes 4194304 | tf_op jit(solution)/shard_map/pallas_call | solution.py:223
  196.1 2.6 shard_map.55
  199.8 2.8 collective-permute-start.1
  202.6 10.7 %collective-permute-done.refs_1_ = bf16[4,2,64,512]{3,2,1,0:T(8,128)(2,1)} collective-permute-done((bf16[4,2,64,512]{3,2,1,0:T(8,128)(2,1)}, bf16[4,2,64,512]{3,2,1,0:T(8,128)(2,1)}, u32[]{:S(2)}, u32[]{:S(2)}) %collective-permute-start) | collective-permute-done | bytes 524320 | tf_op jit(solution)/shard_map/ppermute | solution.py:435
  213.3 12.3 %collective-permute-done.1.refs_2_ = bf16[4,2,64,512]{3,2,1,0:T(8,128)(2,1)} collective-permute-done((bf16[4,2,64,512]{3,2,1,0:T(8,128)(2,1)}, bf16[4,2,64,512]{3,2,1,0:T(8,128)(2,1)}, u32[]{:S(2)}, u32[]{:S(2)}) %collective-permute-start.1) | collective-permute-done | bytes 524320 | tf_op jit(solution)/shard_map/ppermute | solution.py:435
  225.6 2.6 shard_map.56
  228.2 1.3 collective-permute-start.3
  230.0 1.8 collective-permute-start.33
  233.4 4.3 %collective-permute-done.32.one = bf16[3,64,512]{2,1,0:T(8,128)(2,1)S(1)} collective-permute-done((bf16[3,64,512]{2,1,0:T(8,128)(2,1)S(1)}, bf16[3,64,512]{2,1,0:T(8,128)(2,1)S(1)}, u32[]{:S(2)}, u32[]{:S(2)}) %collective-permute-start.32) | collective-permute-done | bytes 196640 | tf_op jit(solution)/shard_map/ppermute | solution.py:329
  237.7 2.9 collective-permute-start.5
  241.2 2.4 collective-permute-start.35
  243.6 29.1 %collective-permute-done.35.recv = bf16[3,64,512]{2,1,0:T(8,128)(2,1)S(1)} collective-permute-done((bf16[3,64,512]{2,1,0:T(8,128)(2,1)S(1)}, bf16[3,64,512]{2,1,0:T(8,128)(2,1)S(1)}, u32[]{:S(2)}, u32[]{:S(2)}) %collective-permute-start.35) | collective-permute-done | bytes 196640 | tf_op jit(solution)/shard_map/ppermute | solution.py:329
  273.6 5.6 %collective-permute-start.38 = (bf16[3,64,512]{2,1,0:T(8,128)(2,1)S(1)}, bf16[3,64,512]{2,1,0:T(8,128)(2,1)S(1)}, u32[]{:S(2)}, u32[]{:S(2)}) collective-permute-start(bf16[3,64,512]{2,1,0:T(8,128)(2,1)S(1)} %get-tuple-element.81.refs_0_), channel_id=1, source_target_pairs={{0,96},{16,112},{32,0},{48,16},{64,32},{80,48},{96,64},{112,80},{1... | collective-permute-start | bytes 589832 | tf_op jit(solution)/shard_map/ppermute | solution.py:329
  279.2 10.8 %collective-permute-start.37 = (bf16[3,64,512]{2,1,0:T(8,128)(2,1)S(1)}, bf16[3,64,512]{2,1,0:T(8,128)(2,1)S(1)}, u32[]{:S(2)}, u32[]{:S(2)}) collective-permute-start(bf16[3,64,512]{2,1,0:T(8,128)(2,1)S(1)} %get-tuple-element.81.refs_0_), channel_id=1, source_target_pairs={{0,64},{16,80},{32,96},{48,112},{64,0},{80,16},{96,32},{112,48},{1... | collective-permute-start | bytes 589832 | tf_op jit(solution)/shard_map/ppermute | solution.py:329
  290.0 1.8 collective-permute-start.39
  292.1 3.4 %collective-permute-start.42 = (bf16[3,64,512]{2,1,0:T(8,128)(2,1)S(1)}, bf16[3,64,512]{2,1,0:T(8,128)(2,1)S(1)}, u32[]{:S(2)}, u32[]{:S(2)}) collective-permute-start(bf16[3,64,512]{2,1,0:T(8,128)(2,1)S(1)} %collective-permute-done.38.refs_3_), channel_id=1, source_target_pairs={{0,16},{16,0},{32,48},{48,32},{64,80},{80,64},{96,112},{112,96},{1... | collective-permute-start | bytes 589832 | tf_op jit(solution)/shard_map/ppermute | solution.py:329
  295.5 2.5 collective-permute-start.41
  298.9 1.4 collective-permute-start.40
  301.2 2.6 shard_map.57.source
  303.8 4.9 %shard_map.58 = (bf16[1024,512]{1,0:T(8,128)(2,1)S(1)}, bf16[1024,512]{1,0:T(8,128)(2,1)S(1)}) custom-call(bf16[16,2,64,512]{3,2,1,0:T(8,128)(2,1)} %shard_map.57.source, bf16[3,2,8,512]{3,2,1,0:T(8,128)(2,1)S(1)} %copy-done.8, bf16[3,2,8,512]{3,2,1,0:T(8,128)(2,1)S(1)} %copy-done.6, bf16[3,2,8,512]{3,2,1,0:T(8,128)(2,1)S(1)} %copy-done.4, ...), custom_call_target="tpu_custom_call" | custom-call | bytes 8388608 | tf_op jit(solution)/shard_map/pallas_call | solution.py:183
  308.7 3.5 %shard_map.75.rest_0_ = bf16[2,1024,512]{2,1,0:T(8,128)(2,1)} custom-call(bf16[1024,512]{1,0:T(8,128)(2,1)S(1)} %get-tuple-element.82.queries, bf16[3,512,512]{2,1,0:T(8,128)(2,1)S(1)} %shard_map.69.weights), custom_call_target="tpu_custom_call" | custom-call | flops 1610612736 | bytes 4194304 | tf_op jit(solution)/shard_map/pallas_call | solution.py:316
  312.4 3.5 %shard_map.76 = bf16[2,1024,512]{2,1,0:T(8,128)(2,1)} custom-call(bf16[1024,512]{1,0:T(8,128)(2,1)S(1)} %get-tuple-element.52.queries, bf16[3,512,512]{2,1,0:T(8,128)(2,1)S(1)} %shard_map.74.weights, bf16[2,1024,512]{2,1,0:T(8,128)(2,1)} %shard_map.75.rest_0_), custom_call_target="tpu_custom_call", output_to_operand_aliasing={{}: (2, {})} | custom-call | flops 1610612736 | bytes 4194304 | tf_op jit(solution)/shard_map/pallas_call | solution.py:316
  (109 shorter events, 24.5 us)
Async XLA Ops:
  2.6 63.3 %all-to-all-start = ((bf16[16,2,64,512]{3,2,1,0:T(8,128)(2,1)}), bf16[16,2,64,512]{3,2,1,0:T(8,128)(2,1)S(1)}, u32[]{:S(2)}, u32[]{:S(2)}) async-start(bf16[16,2,64,512]{3,2,1,0:T(8,128)(2,1)} %shard_map.63), calls=%async_computation | async-start | bytes 4194304 | tf_op jit(solution)/shard_map/all_to_all | solution.py:349
  15.4 2.7 collective-permute-start.6
  16.1 2.0 collective-permute-start.8
  16.8 1.4 collective-permute-start.7
  19.3 3.3 %collective-permute-start.12 = (bf16[3,2,8,512]{3,2,1,0:T(8,128)(2,1)S(1)}, bf16[3,2,8,512]{3,2,1,0:T(8,128)(2,1)S(1)}, u32[]{:S(2)}, u32[]{:S(2)}) collective-permute-start(bf16[3,2,8,512]{3,2,1,0:T(8,128)(2,1)S(1)} %get-tuple-element.86), channel_id=1, source_target_pairs={{3,19},{7,23},{11,27},{15,31},{19,35},{23,39},{27,43},{31,47},{35,... | collective-permute-start | bytes 147464 | tf_op jit(solution)/shard_map/ppermute | solution.py:451
  19.9 2.7 collective-permute-start.11
  20.6 2.0 collective-permute-start.10
  21.3 44.6 %collective-permute-start.9 = (bf16[3,2,8,512]{3,2,1,0:T(8,128)(2,1)S(1)}, bf16[3,2,8,512]{3,2,1,0:T(8,128)(2,1)S(1)}, u32[]{:S(2)}, u32[]{:S(2)}) collective-permute-start(bf16[3,2,8,512]{3,2,1,0:T(8,128)(2,1)S(1)} %get-tuple-element.89), channel_id=1, source_target_pairs={{3,16},{7,20},{11,24},{15,28},{19,32},{23,36},{27,40},{31,44},{35,... | collective-permute-start | bytes 147464 | tf_op jit(solution)/shard_map/ppermute | solution.py:451
  22.6 160.0 %copy-start.1 = (bf16[3,2,8,512]{3,2,1,0:T(8,128)(2,1)}, bf16[3,2,8,512]{3,2,1,0:T(8,128)(2,1)S(1)}, u32[]{:S(2)}) copy-start(bf16[3,2,8,512]{3,2,1,0:T(8,128)(2,1)S(1)} %collective-permute-done.12.rest_3_) | copy-start | bytes 147460
  22.6 160.0 %copy-start.3 = (bf16[3,2,8,512]{3,2,1,0:T(8,128)(2,1)}, bf16[3,2,8,512]{3,2,1,0:T(8,128)(2,1)S(1)}, u32[]{:S(2)}) copy-start(bf16[3,2,8,512]{3,2,1,0:T(8,128)(2,1)S(1)} %collective-permute-done.11.rest_2_) | copy-start | bytes 147460
  22.6 160.0 %copy-start.5 = (bf16[3,2,8,512]{3,2,1,0:T(8,128)(2,1)}, bf16[3,2,8,512]{3,2,1,0:T(8,128)(2,1)S(1)}, u32[]{:S(2)}) copy-start(bf16[3,2,8,512]{3,2,1,0:T(8,128)(2,1)S(1)} %collective-permute-done.10.rest_1_) | copy-start | bytes 147460
  65.9 116.7 %copy-start.7 = (bf16[3,2,8,512]{3,2,1,0:T(8,128)(2,1)}, bf16[3,2,8,512]{3,2,1,0:T(8,128)(2,1)S(1)}, u32[]{:S(2)}) copy-start(bf16[3,2,8,512]{3,2,1,0:T(8,128)(2,1)S(1)} %collective-permute-done.9.rest_0_) | copy-start | bytes 147460
  79.0 37.2 %collective-permute-start.19 = (bf16[4,3,64,512]{3,2,1,0:T(8,128)(2,1)}, bf16[4,3,64,512]{3,2,1,0:T(8,128)(2,1)S(1)}, u32[]{:S(2)}, u32[]{:S(2)}) collective-permute-start(bf16[4,3,64,512]{3,2,1,0:T(8,128)(2,1)} %get-tuple-element.67), channel_id=1, source_target_pairs={{0,16},{16,0},{32,48},{48,32},{64,80},{80,64},{96,112},{112,96},{1... | collective-permute-start | bytes 2359304 | tf_op jit(solution)/shard_map/ppermute | solution.py:329
  85.3 15.0 %collective-permute-start.13 = (bf16[4,2,64,512]{3,2,1,0:T(8,128)(2,1)}, bf16[4,2,64,512]{3,2,1,0:T(8,128)(2,1)S(1)}, u32[]{:S(2)}, u32[]{:S(2)}) collective-permute-start(bf16[4,2,64,512]{3,2,1,0:T(8,128)(2,1)} %get-tuple-element.54), channel_id=1, source_target_pairs={{0,4},{1,5},{2,6},{3,7},{4,8},{5,9},{6,10},{7,11},{8,12},{9,13},{1... | collective-permute-start | bytes 1572872 | tf_op jit(solution)/shard_map/ppermute | solution.py:435
  86.6 25.8 %collective-permute-start.14 = (bf16[4,2,64,512]{3,2,1,0:T(8,128)(2,1)}, bf16[4,2,64,512]{3,2,1,0:T(8,128)(2,1)S(1)}, u32[]{:S(2)}, u32[]{:S(2)}) collective-permute-start(bf16[4,2,64,512]{3,2,1,0:T(8,128)(2,1)} %get-tuple-element.55), channel_id=1, source_target_pairs={{0,8},{1,9},{2,10},{3,11},{4,12},{5,13},{6,14},{7,15},{8,0},{9,1},... | collective-permute-start | bytes 1572872 | tf_op jit(solution)/shard_map/ppermute | solution.py:435
  89.0 23.5 %collective-permute-start.15 = (bf16[4,2,64,512]{3,2,1,0:T(8,128)(2,1)}, bf16[4,2,64,512]{3,2,1,0:T(8,128)(2,1)S(1)}, u32[]{:S(2)}, u32[]{:S(2)}) collective-permute-start(bf16[4,2,64,512]{3,2,1,0:T(8,128)(2,1)} %get-tuple-element.56), channel_id=1, source_target_pairs={{0,12},{1,13},{2,14},{3,15},{4,0},{5,1},{6,2},{7,3},{8,4},{9,5},{1... | collective-permute-start | bytes 1572872 | tf_op jit(solution)/shard_map/ppermute | solution.py:435
  116.0 51.2 %collective-permute-start.16 = (bf16[4,2,64,512]{3,2,1,0:T(8,128)(2,1)}, bf16[4,2,64,512]{3,2,1,0:T(8,128)(2,1)}, u32[]{:S(2)}, u32[]{:S(2)}) collective-permute-start(bf16[4,2,64,512]{3,2,1,0:T(8,128)(2,1)} %get-tuple-element.58), channel_id=1, source_target_pairs={{0,1},{1,2},{2,3},{3,0},{4,5},{5,6},{6,7},{7,4},{8,9},{9,10},{10,1... | collective-permute-start | bytes 1572872 | tf_op jit(solution)/shard_map/ppermute | solution.py:435
  116.3 7.0 %collective-permute-start.20 = (bf16[3,64,512]{2,1,0:T(8,128)(2,1)S(1)}, bf16[3,64,512]{2,1,0:T(8,128)(2,1)S(1)}, u32[]{:S(2)}, u32[]{:S(2)}) collective-permute-start(bf16[3,64,512]{2,1,0:T(8,128)(2,1)S(1)} %get-tuple-element.69), channel_id=1, source_target_pairs={{0,32},{16,48},{32,64},{48,80},{64,96},{80,112},{96,0},{112,16},{1... | collective-permute-start | bytes 589832 | tf_op jit(solution)/shard_map/ppermute | solution.py:329
  116.8 10.7 %collective-permute-start.21 = (bf16[3,64,512]{2,1,0:T(8,128)(2,1)S(1)}, bf16[3,64,512]{2,1,0:T(8,128)(2,1)S(1)}, u32[]{:S(2)}, u32[]{:S(2)}) collective-permute-start(bf16[3,64,512]{2,1,0:T(8,128)(2,1)S(1)} %get-tuple-element.70), channel_id=1, source_target_pairs={{0,64},{16,80},{32,96},{48,112},{64,0},{80,16},{96,32},{112,48},{1... | collective-permute-start | bytes 589832 | tf_op jit(solution)/shard_map/ppermute | solution.py:329
  119.6 8.2 %collective-permute-start.22 = (bf16[3,64,512]{2,1,0:T(8,128)(2,1)S(1)}, bf16[3,64,512]{2,1,0:T(8,128)(2,1)S(1)}, u32[]{:S(2)}, u32[]{:S(2)}) collective-permute-start(bf16[3,64,512]{2,1,0:T(8,128)(2,1)S(1)} %get-tuple-element.71), channel_id=1, source_target_pairs={{0,96},{16,112},{32,0},{48,16},{64,32},{80,48},{96,64},{112,80},{1... | collective-permute-start | bytes 589832 | tf_op jit(solution)/shard_map/ppermute | solution.py:329
  120.5 47.4 %collective-permute-start.17 = (bf16[4,2,64,512]{3,2,1,0:T(8,128)(2,1)}, bf16[4,2,64,512]{3,2,1,0:T(8,128)(2,1)}, u32[]{:S(2)}, u32[]{:S(2)}) collective-permute-start(bf16[4,2,64,512]{3,2,1,0:T(8,128)(2,1)} %get-tuple-element.59), channel_id=1, source_target_pairs={{0,2},{1,3},{2,0},{3,1},{4,6},{5,7},{6,4},{7,5},{8,10},{9,11},{10,... | collective-permute-start | bytes 1572872 | tf_op jit(solution)/shard_map/ppermute | solution.py:435
  127.9 37.1 %collective-permute-start.23 = (bf16[3,64,512]{2,1,0:T(8,128)(2,1)S(1)}, bf16[3,64,512]{2,1,0:T(8,128)(2,1)S(1)}, u32[]{:S(2)}, u32[]{:S(2)}) collective-permute-start(bf16[3,64,512]{2,1,0:T(8,128)(2,1)S(1)} %shard_map.67.mine), channel_id=1, source_target_pairs={{0,128},{16,144},{32,160},{48,176},{64,192},{80,208},{96,224},{112... | collective-permute-start | bytes 589832 | tf_op jit(solution)/shard_map/ppermute | solution.py:329
  131.4 48.6 %collective-permute-start.18 = (bf16[4,2,64,512]{3,2,1,0:T(8,128)(2,1)}, bf16[4,2,64,512]{3,2,1,0:T(8,128)(2,1)}, u32[]{:S(2)}, u32[]{:S(2)}) collective-permute-start(bf16[4,2,64,512]{3,2,1,0:T(8,128)(2,1)} %get-tuple-element.60), channel_id=1, source_target_pairs={{0,3},{1,0},{2,1},{3,2},{4,7},{5,4},{6,5},{7,6},{8,11},{9,8},{10,9... | collective-permute-start | bytes 1572872 | tf_op jit(solution)/shard_map/ppermute | solution.py:435
  165.2 5.4 %collective-permute-start.26 = (bf16[3,64,512]{2,1,0:T(8,128)(2,1)S(1)}, bf16[3,64,512]{2,1,0:T(8,128)(2,1)S(1)}, u32[]{:S(2)}, u32[]{:S(2)}) collective-permute-start(bf16[3,64,512]{2,1,0:T(8,128)(2,1)S(1)} %get-tuple-element.72.refs_0_), channel_id=1, source_target_pairs={{0,96},{16,112},{32,0},{48,16},{64,32},{80,48},{96,64},{112,80},{1... | collective-permute-start | bytes 589832 | tf_op jit(solution)/shard_map/ppermute | solution.py:329
  167.0 9.4 %collective-permute-start.25 = (bf16[3,64,512]{2,1,0:T(8,128)(2,1)S(1)}, bf16[3,64,512]{2,1,0:T(8,128)(2,1)S(1)}, u32[]{:S(2)}, u32[]{:S(2)}) collective-permute-start(bf16[3,64,512]{2,1,0:T(8,128)(2,1)S(1)} %get-tuple-element.72.refs_0_), channel_id=1, source_target_pairs={{0,64},{16,80},{32,96},{48,112},{64,0},{80,16},{96,32},{112,48},{1... | collective-permute-start | bytes 589832 | tf_op jit(solution)/shard_map/ppermute | solution.py:329
  167.2 11.7 %collective-permute-start.24 = (bf16[3,64,512]{2,1,0:T(8,128)(2,1)S(1)}, bf16[3,64,512]{2,1,0:T(8,128)(2,1)S(1)}, u32[]{:S(2)}, u32[]{:S(2)}) collective-permute-start(bf16[3,64,512]{2,1,0:T(8,128)(2,1)S(1)} %get-tuple-element.72.refs_0_), channel_id=1, source_target_pairs={{0,32},{16,48},{32,64},{48,80},{64,96},{80,112},{96,0},{112,16},{1... | collective-permute-start | bytes 589832 | tf_op jit(solution)/shard_map/ppermute | solution.py:329
  167.9 20.1 %collective-permute-start.27 = (bf16[3,64,512]{2,1,0:T(8,128)(2,1)S(1)}, bf16[3,64,512]{2,1,0:T(8,128)(2,1)S(1)}, u32[]{:S(2)}, u32[]{:S(2)}) collective-permute-start(bf16[3,64,512]{2,1,0:T(8,128)(2,1)S(1)} %get-tuple-element.72.refs_0_), channel_id=1, source_target_pairs={{0,16},{16,0},{32,48},{48,32},{64,80},{80,64},{96,112},{112,96},{1... | collective-permute-start | bytes 589832 | tf_op jit(solution)/shard_map/ppermute | solution.py:329
  170.7 17.4 %collective-permute-start.30 = (bf16[3,64,512]{2,1,0:T(8,128)(2,1)S(1)}, bf16[3,64,512]{2,1,0:T(8,128)(2,1)S(1)}, u32[]{:S(2)}, u32[]{:S(2)}) collective-permute-start(bf16[3,64,512]{2,1,0:T(8,128)(2,1)S(1)} %collective-permute-done.26.refs_3_), channel_id=1, source_target_pairs={{0,16},{16,0},{32,48},{48,32},{64,80},{80,64},{96,112},{112,96},{1... | collective-permute-start | bytes 589832 | tf_op jit(solution)/shard_map/ppermute | solution.py:329
  176.4 11.7 %collective-permute-start.29 = (bf16[3,64,512]{2,1,0:T(8,128)(2,1)S(1)}, bf16[3,64,512]{2,1,0:T(8,128)(2,1)S(1)}, u32[]{:S(2)}, u32[]{:S(2)}) collective-permute-start(bf16[3,64,512]{2,1,0:T(8,128)(2,1)S(1)} %collective-permute-done.25.refs_2_), channel_id=1, source_target_pairs={{0,16},{16,0},{32,48},{48,32},{64,80},{80,64},{96,112},{112,96},{1... | collective-permute-start | bytes 589832 | tf_op jit(solution)/shard_map/ppermute | solution.py:329
  178.9 9.2 %collective-permute-start.28 = (bf16[3,64,512]{2,1,0:T(8,128)(2,1)S(1)}, bf16[3,64,512]{2,1,0:T(8,128)(2,1)S(1)}, u32[]{:S(2)}, u32[]{:S(2)}) collective-permute-start(bf16[3,64,512]{2,1,0:T(8,128)(2,1)S(1)} %collective-permute-done.24.refs_1_), channel_id=1, source_target_pairs={{0,16},{16,0},{32,48},{48,32},{64,80},{80,64},{96,112},{112,96},{1... | collective-permute-start | bytes 589832 | tf_op jit(solution)/shard_map/ppermute | solution.py:329
  196.1 33.5 %collective-permute-start.31 = (bf16[4,3,64,512]{3,2,1,0:T(8,128)(2,1)}, bf16[4,3,64,512]{3,2,1,0:T(8,128)(2,1)S(1)}, u32[]{:S(2)}, u32[]{:S(2)}) collective-permute-start(bf16[4,3,64,512]{3,2,1,0:T(8,128)(2,1)} %get-tuple-element.74), channel_id=1, source_target_pairs={{0,16},{16,0},{32,48},{48,32},{64,80},{80,64},{96,112},{112,96},{1... | collective-permute-start | bytes 2359304 | tf_op jit(solution)/shard_map/ppermute | solution.py:329
  198.7 14.6 %collective-permute-start = (bf16[4,2,64,512]{3,2,1,0:T(8,128)(2,1)}, bf16[4,2,64,512]{3,2,1,0:T(8,128)(2,1)}, u32[]{:S(2)}, u32[]{:S(2)}) collective-permute-start(bf16[4,2,64,512]{3,2,1,0:T(8,128)(2,1)} %get-tuple-element.45), channel_id=1, source_target_pairs={{0,4},{1,5},{2,6},{3,7},{4,8},{5,9},{6,10},{7,11},{8,12},{9,13},{1... | collective-permute-start | bytes 1572872 | tf_op jit(solution)/shard_map/ppermute | solution.py:435
  199.8 25.9 %collective-permute-start.1 = (bf16[4,2,64,512]{3,2,1,0:T(8,128)(2,1)}, bf16[4,2,64,512]{3,2,1,0:T(8,128)(2,1)}, u32[]{:S(2)}, u32[]{:S(2)}) collective-permute-start(bf16[4,2,64,512]{3,2,1,0:T(8,128)(2,1)} %get-tuple-element.46), channel_id=1, source_target_pairs={{0,8},{1,9},{2,10},{3,11},{4,12},{5,13},{6,14},{7,15},{8,0},{9,1},... | collective-permute-start | bytes 1572872 | tf_op jit(solution)/shard_map/ppermute | solution.py:435
  202.6 23.1 %collective-permute-start.2 = (bf16[4,2,64,512]{3,2,1,0:T(8,128)(2,1)}, bf16[4,2,64,512]{3,2,1,0:T(8,128)(2,1)}, u32[]{:S(2)}, u32[]{:S(2)}) collective-permute-start(bf16[4,2,64,512]{3,2,1,0:T(8,128)(2,1)} %get-tuple-element.47), channel_id=1, source_target_pairs={{0,12},{1,13},{2,14},{3,15},{4,0},{5,1},{6,2},{7,3},{8,4},{9,5},{1... | collective-permute-start | bytes 1572872 | tf_op jit(solution)/shard_map/ppermute | solution.py:435
  228.2 61.7 %collective-permute-start.3 = (bf16[4,2,64,512]{3,2,1,0:T(8,128)(2,1)}, bf16[4,2,64,512]{3,2,1,0:T(8,128)(2,1)S(1)}, u32[]{:S(2)}, u32[]{:S(2)}) collective-permute-start(bf16[4,2,64,512]{3,2,1,0:T(8,128)(2,1)} %get-tuple-element.49), channel_id=1, source_target_pairs={{0,1},{1,2},{2,3},{3,0},{4,5},{5,6},{6,7},{7,4},{8,9},{9,10},{10,1... | collective-permute-start | bytes 1572872 | tf_op jit(solution)/shard_map/ppermute | solution.py:435
  229.7 8.0 %collective-permute-start.32 = (bf16[3,64,512]{2,1,0:T(8,128)(2,1)S(1)}, bf16[3,64,512]{2,1,0:T(8,128)(2,1)S(1)}, u32[]{:S(2)}, u32[]{:S(2)}) collective-permute-start(bf16[3,64,512]{2,1,0:T(8,128)(2,1)S(1)} %get-tuple-element.76), channel_id=1, source_target_pairs={{0,32},{16,48},{32,64},{48,80},{64,96},{80,112},{96,0},{112,16},{1... | collective-permute-start | bytes 589832 | tf_op jit(solution)/shard_map/ppermute | solution.py:329
  230.0 10.6 %collective-permute-start.33 = (bf16[3,64,512]{2,1,0:T(8,128)(2,1)S(1)}, bf16[3,64,512]{2,1,0:T(8,128)(2,1)S(1)}, u32[]{:S(2)}, u32[]{:S(2)}) collective-permute-start(bf16[3,64,512]{2,1,0:T(8,128)(2,1)S(1)} %get-tuple-element.77), channel_id=1, source_target_pairs={{0,64},{16,80},{32,96},{48,112},{64,0},{80,16},{96,32},{112,48},{1... | collective-permute-start | bytes 589832 | tf_op jit(solution)/shard_map/ppermute | solution.py:329
  231.8 9.3 %collective-permute-start.34 = (bf16[3,64,512]{2,1,0:T(8,128)(2,1)S(1)}, bf16[3,64,512]{2,1,0:T(8,128)(2,1)S(1)}, u32[]{:S(2)}, u32[]{:S(2)}) collective-permute-start(bf16[3,64,512]{2,1,0:T(8,128)(2,1)S(1)} %get-tuple-element.78), channel_id=1, source_target_pairs={{0,96},{16,112},{32,0},{48,16},{64,32},{80,48},{96,64},{112,80},{1... | collective-permute-start | bytes 589832 | tf_op jit(solution)/shard_map/ppermute | solution.py:329
  232.7 57.3 %collective-permute-start.4 = (bf16[4,2,64,512]{3,2,1,0:T(8,128)(2,1)}, bf16[4,2,64,512]{3,2,1,0:T(8,128)(2,1)S(1)}, u32[]{:S(2)}, u32[]{:S(2)}) collective-permute-start(bf16[4,2,64,512]{3,2,1,0:T(8,128)(2,1)} %get-tuple-element.50), channel_id=1, source_target_pairs={{0,2},{1,3},{2,0},{3,1},{4,6},{5,7},{6,4},{7,5},{8,10},{9,11},{10,... | collective-permute-start | bytes 1572872 | tf_op jit(solution)/shard_map/ppermute | solution.py:435
  237.7 62.6 %collective-permute-start.5 = (bf16[4,2,64,512]{3,2,1,0:T(8,128)(2,1)}, bf16[4,2,64,512]{3,2,1,0:T(8,128)(2,1)S(1)}, u32[]{:S(2)}, u32[]{:S(2)}) collective-permute-start(bf16[4,2,64,512]{3,2,1,0:T(8,128)(2,1)} %get-tuple-element.51), channel_id=1, source_target_pairs={{0,3},{1,0},{2,1},{3,2},{4,7},{5,4},{6,5},{7,6},{8,11},{9,8},{10,9... | collective-permute-start | bytes 1572872 | tf_op jit(solution)/shard_map/ppermute | solution.py:435
  241.2 31.4 %collective-permute-start.35 = (bf16[3,64,512]{2,1,0:T(8,128)(2,1)S(1)}, bf16[3,64,512]{2,1,0:T(8,128)(2,1)S(1)}, u32[]{:S(2)}, u32[]{:S(2)}) collective-permute-start(bf16[3,64,512]{2,1,0:T(8,128)(2,1)S(1)} %shard_map.72.mine), channel_id=1, source_target_pairs={{0,128},{16,144},{32,160},{48,176},{64,192},{80,208},{96,224},{112... | collective-permute-start | bytes 589832 | tf_op jit(solution)/shard_map/ppermute | solution.py:329
  273.6 18.5 %collective-permute-start.38 = (bf16[3,64,512]{2,1,0:T(8,128)(2,1)S(1)}, bf16[3,64,512]{2,1,0:T(8,128)(2,1)S(1)}, u32[]{:S(2)}, u32[]{:S(2)}) collective-permute-start(bf16[3,64,512]{2,1,0:T(8,128)(2,1)S(1)} %get-tuple-element.81.refs_0_), channel_id=1, source_target_pairs={{0,96},{16,112},{32,0},{48,16},{64,32},{80,48},{96,64},{112,80},{1... | collective-permute-start | bytes 589832 | tf_op jit(solution)/shard_map/ppermute | solution.py:329
  279.2 16.4 %collective-permute-start.37 = (bf16[3,64,512]{2,1,0:T(8,128)(2,1)S(1)}, bf16[3,64,512]{2,1,0:T(8,128)(2,1)S(1)}, u32[]{:S(2)}, u32[]{:S(2)}) collective-permute-start(bf16[3,64,512]{2,1,0:T(8,128)(2,1)S(1)} %get-tuple-element.81.refs_0_), channel_id=1, source_target_pairs={{0,64},{16,80},{32,96},{48,112},{64,0},{80,16},{96,32},{112,48},{1... | collective-permute-start | bytes 589832 | tf_op jit(solution)/shard_map/ppermute | solution.py:329
  289.9 8.9 %collective-permute-start.36 = (bf16[3,64,512]{2,1,0:T(8,128)(2,1)S(1)}, bf16[3,64,512]{2,1,0:T(8,128)(2,1)S(1)}, u32[]{:S(2)}, u32[]{:S(2)}) collective-permute-start(bf16[3,64,512]{2,1,0:T(8,128)(2,1)S(1)} %get-tuple-element.81.refs_0_), channel_id=1, source_target_pairs={{0,32},{16,48},{32,64},{48,80},{64,96},{80,112},{96,0},{112,16},{1... | collective-permute-start | bytes 589832 | tf_op jit(solution)/shard_map/ppermute | solution.py:329
  290.0 22.3 %collective-permute-start.39 = (bf16[3,64,512]{2,1,0:T(8,128)(2,1)S(1)}, bf16[3,64,512]{2,1,0:T(8,128)(2,1)S(1)}, u32[]{:S(2)}, u32[]{:S(2)}) collective-permute-start(bf16[3,64,512]{2,1,0:T(8,128)(2,1)S(1)} %get-tuple-element.81.refs_0_), channel_id=1, source_target_pairs={{0,16},{16,0},{32,48},{48,32},{64,80},{80,64},{96,112},{112,96},{1... | collective-permute-start | bytes 589832 | tf_op jit(solution)/shard_map/ppermute | solution.py:329
  292.1 20.2 %collective-permute-start.42 = (bf16[3,64,512]{2,1,0:T(8,128)(2,1)S(1)}, bf16[3,64,512]{2,1,0:T(8,128)(2,1)S(1)}, u32[]{:S(2)}, u32[]{:S(2)}) collective-permute-start(bf16[3,64,512]{2,1,0:T(8,128)(2,1)S(1)} %collective-permute-done.38.refs_3_), channel_id=1, source_target_pairs={{0,16},{16,0},{32,48},{48,32},{64,80},{80,64},{96,112},{112,96},{1... | collective-permute-start | bytes 589832 | tf_op jit(solution)/shard_map/ppermute | solution.py:329
  295.5 16.7 %collective-permute-start.41 = (bf16[3,64,512]{2,1,0:T(8,128)(2,1)S(1)}, bf16[3,64,512]{2,1,0:T(8,128)(2,1)S(1)}, u32[]{:S(2)}, u32[]{:S(2)}) collective-permute-start(bf16[3,64,512]{2,1,0:T(8,128)(2,1)S(1)} %collective-permute-done.37.refs_2_), channel_id=1, source_target_pairs={{0,16},{16,0},{32,48},{48,32},{64,80},{80,64},{96,112},{112,96},{1... | collective-permute-start | bytes 589832 | tf_op jit(solution)/shard_map/ppermute | solution.py:329
  298.9 13.4 %collective-permute-start.40 = (bf16[3,64,512]{2,1,0:T(8,128)(2,1)S(1)}, bf16[3,64,512]{2,1,0:T(8,128)(2,1)S(1)}, u32[]{:S(2)}, u32[]{:S(2)}) collective-permute-start(bf16[3,64,512]{2,1,0:T(8,128)(2,1)S(1)} %collective-permute-done.36.refs_1_), channel_id=1, source_target_pairs={{0,16},{16,0},{32,48},{48,32},{64,80},{80,64},{96,112},{112,96},{1... | collective-permute-start | bytes 589832 | tf_op jit(solution)/shard_map/ppermute | solution.py:329
  (17 other events, 216.8 us)
